TPU v7x, 32 devices: a whole 2x2x4 slice. The times are simulated.
32 devices in a mesh: expert: 16 (over z, y, x), replica: 2 (over core).
Axes of the slice: x: 2, y: 2, z: 4, core: 2. Of those that a mesh axis runs over, the one named last changes fastest.
Arguments:
- tokens: bfloat16 [1024, 7168], P('expert', 'replica'), may hold values from -6 to 6
- routes: int32 [1024, 8], P('expert'), may hold values from 0 to 15, all different within a row; in each aligned block of 64 rows (0 to 63, 64 to 127, ...) at most 64 rows name the same one
- route_scores: float32 [1024, 8], P('expert'), may hold values from 0.05 to 1
- placement: int32 [16], replicated, may hold values from 0 to 15, each once
- w_in: bfloat16 [16, 7168, 2, 1024], P('expert', 'replica'), may hold values from -0.0625 to 0.0625
- w_out: bfloat16 [16, 1024, 7168], P('expert', None, 'replica'), may hold values from -0.1875 to 0.1875
Outputs:
- mixed: bfloat16 [1024, 7168], P('expert', 'replica')
Inputs may be any that keep to these rules, and one draw needn't show every extreme that they name: `routes`: each row names 8 different logical experts. Among the 64 rows of each aligned block (the tokens of one index of the expert axis) no expert is named by more than 64 rows, a bound that some block reaches. `placement`: A permutation of the physical slots.
All inputs are finite; a program needn't handle non-finite values.
Results may differ from a plain program's by a relative error of at most 0.0057.
Values may be sent and summed in bfloat16 or wider, within the bound.
A program may use at most 128 MiB of HBM per device.

v0:
```python
import jax
import jax.numpy as jnp
from jax import lax
from jax.experimental import pallas as pl
from jax.experimental.pallas import tpu as pltpu
from jax.sharding import PartitionSpec as P

LANES = 128
TILE = 256
MESH = pl.DeviceIdType.MESH
LINE = 4


def packed(tokens, routes, route_scores, placement, w_in, w_out):
    tok_rows, feature_cols = tokens.shape
    route_count = routes.shape[1]
    experts = placement.shape[0]
    hidden_units = w_in.shape[3]
    capacity = min(tok_rows, max(2, 2 * tok_rows * route_count // experts))
    slot_total = experts * capacity
    expert_ids = jnp.arange(experts, dtype=jnp.int32)
    route_table = routes[:, :, None] == expert_ids
    physical = jnp.sum(jnp.where(route_table, placement, 0), axis=-1)
    flat_slots = physical.reshape(-1)
    onehot = (flat_slots[:, None] == expert_ids).astype(jnp.int32)
    earlier = jnp.sum((jnp.cumsum(onehot, axis=0) - onehot) * onehot, axis=1)
    position = (flat_slots * capacity + earlier).reshape(tok_rows, route_count)
    slot_index = jnp.arange(slot_total, dtype=jnp.int32)
    placing = jnp.any(position[None, :, :] == slot_index[:, None, None], axis=-1).astype(
        jnp.bfloat16
    )
    outgoing = jnp.dot(placing, tokens, preferred_element_type=jnp.float32).astype(jnp.bfloat16)
    incoming = lax.all_to_all(outgoing, "expert", split_axis=0, concat_axis=0, tiled=True)
    weights_in = w_in[0].reshape(feature_cols, 2 * hidden_units)
    weights_out = w_out[0]
    partial_value = jnp.dot(incoming, weights_in, preferred_element_type=jnp.float32)
    partial_value = partial_value.reshape(slot_total, 2, hidden_units)
    shares = lax.psum_scatter(partial_value, "replica", scatter_dimension=2, tiled=True)
    active = (jax.nn.silu(shares[:, 0]) * shares[:, 1]).astype(jnp.bfloat16)
    result = jnp.dot(
        lax.all_gather(active, "replica", axis=1, tiled=True),
        weights_out,
        preferred_element_type=jnp.float32,
    )
    expert_out = result.astype(jnp.bfloat16)
    returned = lax.all_to_all(expert_out, "expert", split_axis=0, concat_axis=0, tiled=True)
    route_weight = 2.5 * route_scores / jnp.sum(route_scores, axis=1, keepdims=True)
    picked = returned[position.reshape(-1)].reshape(tok_rows, route_count, feature_cols)
    mixed = jnp.sum(picked.astype(jnp.float32) * route_weight[:, :, None], axis=1)
    return mixed.astype(jnp.bfloat16)


def expert_weights(routes, route_scores, placement):
    experts = placement.shape[0]
    expert_ids = jnp.arange(experts, dtype=jnp.int32)
    physical = jnp.sum(jnp.where(routes[:, :, None] == expert_ids, placement, 0), axis=-1)
    route_weight = 2.5 * route_scores / jnp.sum(route_scores, axis=1, keepdims=True)
    return jnp.sum(
        jnp.where(physical[:, :, None] == expert_ids, route_weight[:, :, None], 0.0), axis=1
    )


def layer_kernel(
    ext_ref, w_in_ref, w_out_ref, out_ref,
    xs, wg, wu, stage, wo, contrib, from_b, from_a, from_z, part, sent, got, act,
    w_sem, wo_sem, z_send, a_send, b_send, x_recv,
    p_send, p_recv, rb_send, rb_recv, ra_send, ra_recv, rz_send, rz_recv,
):
    rows, width = ext_ref.shape
    cols = out_ref.shape[1]
    hidden = wg.shape[1]
    tiles = hidden // TILE
    me = lax.axis_index("expert")
    core = lax.axis_index("replica")
    x, y, z = me % 2, (me // 2) % 2, me // 4
    flip_x, flip_y = me + 1 - 2 * x, me + 2 - 4 * y
    near_a = (1 - core) * flip_x + core * flip_y
    near_b = (1 - core) * flip_y + core * flip_x
    base = me - 4 * z

    def line(d):
        return (z + d) % LINE

    barrier = pltpu.get_barrier_semaphore()
    peers = [(near_a, core), (near_b, core), (me, 1 - core)]
    peers += [(base + 4 * line(d), core) for d in range(1, LINE)]
    for peer in peers:
        pl.semaphore_signal(barrier, inc=1, device_id=peer, device_id_type=MESH)
    pl.semaphore_wait(barrier, len(peers))

    def remote(src, dst, send, recv, chip, on_core=None):
        return pltpu.make_async_remote_copy(
            src_ref=src, dst_ref=dst, send_sem=send, recv_sem=recv,
            device_id=(chip, core if on_core is None else on_core), device_id_type=MESH,
        )

    def arrived(ref, recv):
        remote(ref, ref, a_send.at[0, 0], recv, near_a).wait_recv()

    def stage_copy(ct):
        return pltpu.make_async_copy(
            w_in_ref.at[0, :, :, pl.ds(ct * LANES, LANES)], stage.at[ct % 2], w_sem.at[ct % 2]
        )

    pending = []

    def go(copy):
        copy.start()
        pending.append(copy)

    part_rows = rows // 2

    def pass_on(source, to, send, chip, h):
        part = pl.ds(h * part_rows, part_rows)
        go(remote(source, xs.at[to, part], send.at[h], x_recv.at[to, h], chip))

    def landed(slot, h):
        part = pl.ds(h * part_rows, part_rows)
        arrived(xs.at[slot, part], x_recv.at[slot, h])
        return xs.at[slot, part]

    for h in range(2):
        own = ext_ref.at[pl.ds(h * part_rows, part_rows)]
        pass_on(own, LINE + z, a_send.at[0], near_a, h)
        pass_on(own, 2 * LINE + z, b_send.at[0], near_b, h)
        for d in (1, 3, 2):
            pass_on(own, z, z_send.at[d - 1], base + 4 * line(d), h)
    stage_copy(0).start()
    stage_copy(1).start()
    out_weights = pltpu.make_async_copy(w_out_ref.at[0], wo, wo_sem)
    out_weights.start()
    xs[z] = ext_ref[...]

    row = lax.broadcasted_iota(jnp.int32, (TILE, TILE), 0)
    col = lax.broadcasted_iota(jnp.int32, (TILE, TILE), 1)
    half = TILE // 2
    wanted = jnp.where(row < half, 2 * row, 2 * (row - half) + 1)
    sorter = (col == wanted).astype(jnp.float32).astype(jnp.bfloat16)

    def sort_tile(ct):
        stage_copy(ct).wait()
        flat = stage.at[ct % 2].reshape(2 * cols, LANES)

        def body(k, carry):
            piece = flat[pl.ds(pl.multiple_of(k * TILE, TILE), TILE), :]
            both = jnp.dot(sorter, piece, preferred_element_type=jnp.float32).astype(jnp.bfloat16)
            at = pl.ds(pl.multiple_of(k * half, half), half)
            wg[at, ct * LANES:(ct + 1) * LANES] = both[:half]
            wu[at, ct * LANES:(ct + 1) * LANES] = both[half:]
            return carry

        lax.fori_loop(0, 2 * cols // TILE, body, 0)
        if ct + 2 < hidden // LANES:
            stage_copy(ct + 2).start()

    def own_line_on(d, n):
        slot = line(d)
        for h in range(2):
            held = landed(slot, h)
            pass_on(held, LINE + slot, a_send.at[n], near_a, h)
            pass_on(held, 2 * LINE + slot, b_send.at[n], near_b, h)

    def a_line_on(d, n):
        slot = LINE + line(d)
        for h in range(2):
            held = landed(slot, h)
            pass_on(held, 2 * LINE + slot, b_send.at[LINE + n], near_b, h)

    all_tiles = list(range(hidden // LANES))
    quarter = max(1, len(all_tiles) // 4)
    for ct in all_tiles[:2 * quarter]:
        sort_tile(ct)
    own_line_on(1, 1)
    a_line_on(0, 0)
    for ct in all_tiles[2 * quarter:3 * quarter]:
        sort_tile(ct)
    own_line_on(3, 2)
    a_line_on(1, 1)
    for ct in all_tiles[3 * quarter:]:
        sort_tile(ct)
    own_line_on(2, 3)
    a_line_on(3, 2)
    a_line_on(2, 3)
    out_weights.wait()

    lane = lax.broadcasted_iota(jnp.int32, (LINE * rows, LANES), 1)
    mine = (lane % 16 == me) & (lane < 48)

    def exchange(s, j):
        return remote(sent.at[s, j], got.at[s, j], p_send.at[s, j], p_recv.at[s, j], me, 1 - core)

    def step(s, group, ship=None):
        block = pl.ds(group * LINE, LINE)

        def first(j, carry):
            at = pl.ds(pl.multiple_of(j * TILE, TILE), TILE)
            value = xs[block, :, :cols].reshape(LINE * rows, cols)
            gate = jnp.dot(value, wg[:, at], preferred_element_type=jnp.float32)
            up = jnp.dot(value, wu[:, at], preferred_element_type=jnp.float32)
            part[j, 0] = gate
            part[j, 1] = up
            sent[s, j, 0] = gate.astype(jnp.bfloat16)
            sent[s, j, 1] = up.astype(jnp.bfloat16)
            exchange(s, j).start()
            return carry

        lax.fori_loop(0, tiles, first, 0)

        def second(j, carry):
            exchange(s, j).wait_recv()
            gate = part[j, 0] + got[s, j, 0].astype(jnp.float32)
            up = part[j, 1] + got[s, j, 1].astype(jnp.float32)
            act[:, pl.ds(pl.multiple_of(j * TILE, TILE), TILE)] = (
                gate / (1.0 + jnp.exp(-gate)) * up
            ).astype(jnp.bfloat16)
            return carry

        lax.fori_loop(0, tiles, second, 0)
        scales = xs[block, :, cols:].reshape(LINE * rows, LANES).astype(jnp.float32)
        scale = jnp.sum(jnp.where(mine, scales, 0.0), axis=1, keepdims=True)

        def third(j, carry):
            at = pl.ds(pl.multiple_of(j * TILE, TILE), TILE)
            value = jnp.dot(act[...], wo[:, at], preferred_element_type=jnp.float32)
            value = value * scale
            contrib[block, :, at] = value.astype(jnp.bfloat16).reshape(LINE, rows, TILE)
            return carry

        out_tiles = wide // TILE
        for h in range(2):
            lax.fori_loop(h * out_tiles, (h + 1) * out_tiles, third, 0)
            if ship is not None:
                ship(h)

    wide = cols // 2
    order = (1, 3, 2, 0)

    def cut(h):
        return slice(h * wide, (h + 1) * wide)

    def ship_b(from_line, to_line, h):
        for n, d in enumerate(order):
            src, to = from_line * LINE + line(d), to_line * LINE + line(d)
            go(remote(contrib.at[src, :, cut(h)], from_b.at[to, :, cut(h)],
                      rb_send.at[to_line * LINE + n, h], rb_recv.at[to, h], near_b))

    step(0, 0)
    for d in range(LINE):
        for h in range(2):
            landed(2 * LINE + line(d), h)
    step(1, 1 + core)
    step(2, 2 - core)
    for h in range(2):
        ship_b(2, 0, h)
    for d in range(LINE):
        for h in range(2):
            landed(3 * LINE + line(d), h)
    step(3, 3, lambda h: ship_b(3, 1, h))

    def plus(values):
        total = values[0].astype(jnp.float32)
        for value in values[1:]:
            total = total + value.astype(jnp.float32)
        return total

    def to_a(h, n, d):
        slot, to = LINE + line(d), line(d)
        arrived(from_b.at[slot, :, cut(h)], rb_recv.at[slot, h])
        contrib[slot, :, cut(h)] = plus(
            [contrib[slot, :, cut(h)], from_b[slot, :, cut(h)]]
        ).astype(jnp.bfloat16)
        go(remote(contrib.at[slot, :, cut(h)], from_a.at[to, :, cut(h)],
                  ra_send.at[n, h], ra_recv.at[to, h], near_a))

    def to_z(h, n, d):
        slot = line(d)
        arrived(from_b.at[slot, :, cut(h)], rb_recv.at[slot, h])
        arrived(from_a.at[slot, :, cut(h)], ra_recv.at[slot, h])
        contrib[slot, :, cut(h)] = plus(
            [contrib[slot, :, cut(h)], from_b[slot, :, cut(h)], from_a[slot, :, cut(h)]]
        ).astype(jnp.bfloat16)
        if d:
            to = LINE - 1 - d
            go(remote(contrib.at[slot, :, cut(h)], from_z.at[to, :, cut(h)],
                      rz_send.at[n, h], rz_recv.at[to, h], base + 4 * slot))

    for n, d in enumerate(order):
        to_a(0, n, d)
    for n, d in enumerate(order):
        to_a(1, n, d)
        to_z(0, n, d)
    for n, d in enumerate(order):
        to_z(1, n, d)
    for h in range(2):
        for d in range(LINE - 1):
            arrived(from_z.at[d, :, cut(h)], rz_recv.at[d, h])
        out_ref[:, cut(h)] = plus(
            [contrib[z, :, cut(h)]] + [from_z[d, :, cut(h)] for d in range(LINE - 1)]
        ).astype(jnp.bfloat16)
    for copy in pending:
        copy.wait_send()

    def drain(n, carry):
        exchange(n // tiles, n % tiles).wait_send()
        return carry

    lax.fori_loop(0, LINE * tiles, drain, 0)


def fused(tokens, routes, route_scores, placement, w_in, w_out):
    rows, cols = tokens.shape
    hidden = w_in.shape[3]
    tiles = hidden // TILE
    table = expert_weights(routes, route_scores, placement)
    high = lax.reduce_precision(table, 8, 7)
    middle = lax.reduce_precision(table - high, 8, 7)
    low = table - high - middle
    thirds = [third.astype(jnp.bfloat16) for third in (high, middle, low)]
    filler = jnp.zeros((rows, LANES - 3 * table.shape[1]), jnp.bfloat16)
    ext = jnp.concatenate([tokens, *thirds, filler], axis=1)
    slots = LINE * LINE
    bf16 = jnp.bfloat16
    dma = pltpu.SemaphoreType.DMA
    return pl.pallas_call(
        layer_kernel,
        out_shape=jax.ShapeDtypeStruct((rows, cols), bf16),
        in_specs=[
            pl.BlockSpec(memory_space=pltpu.VMEM),
            pl.BlockSpec(memory_space=pl.ANY),
            pl.BlockSpec(memory_space=pl.ANY),
        ],
        out_specs=pl.BlockSpec(memory_space=pltpu.VMEM),
        scratch_shapes=[
            pltpu.VMEM((slots, rows, cols + LANES), bf16),
            pltpu.VMEM((cols, hidden), bf16),
            pltpu.VMEM((cols, hidden), bf16),
            pltpu.VMEM((2, cols, 2, LANES), bf16),
            pltpu.VMEM((hidden, cols), bf16),
            pltpu.VMEM((slots, rows, cols), bf16),
            pltpu.VMEM((2 * LINE, rows, cols), bf16),
            pltpu.VMEM((LINE, rows, cols), bf16),
            pltpu.VMEM((LINE - 1, rows, cols), bf16),
            pltpu.VMEM((tiles, 2, LINE * rows, TILE), jnp.float32),
            pltpu.VMEM((LINE, tiles, 2, LINE * rows, TILE), bf16),
            pltpu.VMEM((LINE, tiles, 2, LINE * rows, TILE), bf16),
            pltpu.VMEM((LINE * rows, hidden), bf16),
            dma((2,)), dma, dma((LINE - 1, 2)), dma((LINE, 2)), dma((2 * LINE, 2)), dma((slots, 2)),
            dma((LINE, tiles)), dma((LINE, tiles)),
            dma((2 * LINE, 2)), dma((2 * LINE, 2)), dma((LINE, 2)), dma((LINE, 2)),
            dma((LINE, 2)), dma((LINE - 1, 2)),
        ],
        compiler_params=pltpu.CompilerParams(
            collective_id=0, has_side_effects=True, vmem_limit_bytes=67043328
        ),
    )(ext, w_in, w_out)


def on_device(tokens, routes, route_scores, placement, w_in, w_out):
    tok_rows = tokens.shape[0]
    experts = placement.shape[0]
    fits = experts == 4 * LINE and lax.axis_size("replica") == 2
    if fits and 2 * tok_rows * routes.shape[1] // experts >= tok_rows:
        return fused(tokens, routes, route_scores, placement, w_in, w_out)
    return packed(tokens, routes, route_scores, placement, w_in, w_out)


def solution(mesh):
    in_specs = (
        P("expert", "replica"),
        P("expert", None),
        P("expert", None),
        P(),
        P("expert", "replica", None, None),
        P("expert", None, "replica"),
    )
    out_specs = P("expert", "replica")
    return jax.shard_map(
        on_device, mesh=mesh, in_specs=in_specs, out_specs=out_specs, check_vma=False
    )
```

profile of v0, /device:TPU:8, one launch (start us, length us, event | category | flops | bytes accessed | tf_op | source)
XLA Modules:
  0.0 190.3 jit_solution(8599562670869001218)
XLA Ops:
  0.0 0.7 reduce_sum.28
  0.7 0.7 multiply_divide_fusion
  1.4 0.8 select_reduce_fusion.1
  2.2 0.1 copy.12
  2.3 0.1 copy.11
  2.4 1.9 concatenate.3.ext_ref
  4.3 184.2 %shard_map.64 = bf16[64,3584]{1,0:T(8,128)(2,1)} custom-call(bf16[64,3712]{1,0:T(8,128)(2,1)} %concatenate.3.ext_ref, bf16[1,3584,2,1024]{3,2,1,0:T(2,128)(2,1)} %w_in_ref.1, bf16[1,1024,3584]{2,1,0:T(8,128)(2,1)} %w_out_ref.1), custom_call_target="tpu_custom_call" | custom-call | tf_op jit(solution)/shard_map/pallas_call | solution.py:324
  188.5 1.8 copy.15
  (4 shorter events, 0.0 us)
where the time goes:
time: 194 us; the launch traced here: 190 us
  Pallas kernels  184 us (95%)
  local copies, waits for them, and re-layouts  3.87 us (2%)
  other arithmetic  2.22 us (1%)
    pallas_call x1, Pallas kernels, fused(): pl.pallas_call(layer_kernel, out_shape=jax.ShapeDtypeStruct((rows, cols),...  184 us

commit v1 on v0

--- a/solution.py
+++ b/solution.py
@@ -131,25 +131,19 @@
     out_weights.start()
     xs[z] = ext_ref[...]
 
-    row = lax.broadcasted_iota(jnp.int32, (TILE, TILE), 0)
-    col = lax.broadcasted_iota(jnp.int32, (TILE, TILE), 1)
     half = TILE // 2
-    wanted = jnp.where(row < half, 2 * row, 2 * (row - half) + 1)
-    sorter = (col == wanted).astype(jnp.float32).astype(jnp.bfloat16)
 
     def sort_tile(ct):
         stage_copy(ct).wait()
-        flat = stage.at[ct % 2].reshape(2 * cols, LANES)
+        at_cols = slice(ct * LANES, (ct + 1) * LANES)
 
         def body(k, carry):
-            piece = flat[pl.ds(pl.multiple_of(k * TILE, TILE), TILE), :]
-            both = jnp.dot(sorter, piece, preferred_element_type=jnp.float32).astype(jnp.bfloat16)
             at = pl.ds(pl.multiple_of(k * half, half), half)
-            wg[at, ct * LANES:(ct + 1) * LANES] = both[:half]
-            wu[at, ct * LANES:(ct + 1) * LANES] = both[half:]
+            wg[at, at_cols] = stage[ct % 2, at, 0, :]
+            wu[at, at_cols] = stage[ct % 2, at, 1, :]
             return carry
 
-        lax.fori_loop(0, 2 * cols // TILE, body, 0)
+        lax.fori_loop(0, cols // half, body, 0)
         if ct + 2 < hidden // LANES:
             stage_copy(ct + 2).start()
 

time: 194 us -> 193 us (level)
  no operation moved by 1% of the time
where the time goes in v1:
time: 193 us; the launch traced here: 189 us
  Pallas kernels  183 us (95%)
  local copies, waits for them, and re-layouts  3.87 us (2%)
  other arithmetic  2.22 us (1%)
    pallas_call x1, Pallas kernels, fused(): pl.pallas_call(layer_kernel, out_shape=jax.ShapeDtypeStruct((rows, cols),...  183 us

profile of v1, /device:TPU:8, one launch (start us, length us, event | category | flops | bytes accessed | tf_op | source)
XLA Modules:
  0.0 189.3 jit_solution(15909120809365557516)
XLA Ops:
  0.0 0.7 reduce_sum.28
  0.7 0.7 multiply_divide_fusion
  1.4 0.8 select_reduce_fusion.1
  2.2 0.1 copy.12
  2.3 0.1 copy.11
  2.4 1.9 concatenate.3.ext_ref
  4.3 183.2 %shard_map.64 = bf16[64,3584]{1,0:T(8,128)(2,1)} custom-call(bf16[64,3712]{1,0:T(8,128)(2,1)} %concatenate.3.ext_ref, bf16[1,3584,2,1024]{3,2,1,0:T(2,128)(2,1)} %w_in_ref.1, bf16[1,1024,3584]{2,1,0:T(8,128)(2,1)} %w_out_ref.1), custom_call_target="tpu_custom_call" | custom-call | tf_op jit(solution)/shard_map/pallas_call | solution.py:318
  187.5 1.8 copy.15
  (4 shorter events, 0.0 us)

commit v2 on v1

v2 whole, which is shorter than its diff:
```python
import functools

import jax
import jax.numpy as jnp
from jax import lax
from jax.experimental import pallas as pl
from jax.experimental.pallas import tpu as pltpu
from jax.sharding import PartitionSpec as P

LANES = 128
TILE = 256
WIDE_TILE = 512
MESH = pl.DeviceIdType.MESH
LINE = 4
OWN, SIDE_A, SIDE_B, DIAGONAL = range(4)
UP, DOWN = range(2)
TO_A, TO_B, TO_UP, TO_DOWN = range(4)
NEAREST = ((0, 1, 2, 3), (1, 0, 2, 3), (2, 3, 1, 0), (3, 2, 1, 0))
ENDS, INNER, EVERY = (0, LINE - 1), (1, 2), (0, 1, 2, 3)


def slot_of(line, rank):
    if line == OWN:
        return rank
    if line == DIAGONAL:
        return 3 * LINE + rank
    return LINE * (1 + rank // 2) + 2 * (line - 1) + rank % 2


def packed(tokens, routes, route_scores, placement, w_in, w_out):
    tok_rows, feature_cols = tokens.shape
    route_count = routes.shape[1]
    experts = placement.shape[0]
    hidden_units = w_in.shape[3]
    capacity = min(tok_rows, max(2, 2 * tok_rows * route_count // experts))
    slot_total = experts * capacity
    expert_ids = jnp.arange(experts, dtype=jnp.int32)
    route_table = routes[:, :, None] == expert_ids
    physical = jnp.sum(jnp.where(route_table, placement, 0), axis=-1)
    flat_slots = physical.reshape(-1)
    onehot = (flat_slots[:, None] == expert_ids).astype(jnp.int32)
    earlier = jnp.sum((jnp.cumsum(onehot, axis=0) - onehot) * onehot, axis=1)
    position = (flat_slots * capacity + earlier).reshape(tok_rows, route_count)
    slot_index = jnp.arange(slot_total, dtype=jnp.int32)
    placing = jnp.any(position[None, :, :] == slot_index[:, None, None], axis=-1).astype(
        jnp.bfloat16
    )
    outgoing = jnp.dot(placing, tokens, preferred_element_type=jnp.float32).astype(jnp.bfloat16)
    incoming = lax.all_to_all(outgoing, "expert", split_axis=0, concat_axis=0, tiled=True)
    weights_in = w_in[0].reshape(feature_cols, 2 * hidden_units)
    weights_out = w_out[0]
    partial_value = jnp.dot(incoming, weights_in, preferred_element_type=jnp.float32)
    partial_value = partial_value.reshape(slot_total, 2, hidden_units)
    shares = lax.psum_scatter(partial_value, "replica", scatter_dimension=2, tiled=True)
    active = (jax.nn.silu(shares[:, 0]) * shares[:, 1]).astype(jnp.bfloat16)
    result = jnp.dot(
        lax.all_gather(active, "replica", axis=1, tiled=True),
        weights_out,
        preferred_element_type=jnp.float32,
    )
    expert_out = result.astype(jnp.bfloat16)
    returned = lax.all_to_all(expert_out, "expert", split_axis=0, concat_axis=0, tiled=True)
    route_weight = 2.5 * route_scores / jnp.sum(route_scores, axis=1, keepdims=True)
    picked = returned[position.reshape(-1)].reshape(tok_rows, route_count, feature_cols)
    mixed = jnp.sum(picked.astype(jnp.float32) * route_weight[:, :, None], axis=1)
    return mixed.astype(jnp.bfloat16)


def expert_weights(routes, route_scores, placement):
    experts = placement.shape[0]
    expert_ids = jnp.arange(experts, dtype=jnp.int32)
    physical = jnp.sum(jnp.where(routes[:, :, None] == expert_ids, placement, 0), axis=-1)
    route_weight = 2.5 * route_scores / jnp.sum(route_scores, axis=1, keepdims=True)
    return jnp.sum(
        jnp.where(physical[:, :, None] == expert_ids, route_weight[:, :, None], 0.0), axis=1
    )


def layer_kernel(
    ext_ref, w_in_ref, w_out_ref, out_ref,
    xs, wg, wu, stage, wo, contrib, z_in, a_in, b_in, part, sent, got, act,
    w_sem, wo_sem, x_send, x_recv, p_send, p_recv,
    z_send, z_recv, a_send, a_recv, b_send, b_recv,
):
    rows, width = ext_ref.shape
    cols = out_ref.shape[1]
    hidden = wg.shape[1]
    tiles = hidden // TILE
    me = lax.axis_index("expert")
    core = lax.axis_index("replica")
    x, y, z = me % 2, (me // 2) % 2, me // 4
    flip_x, flip_y = me + 1 - 2 * x, me + 2 - 4 * y
    near_a = (1 - core) * flip_x + core * flip_y
    near_b = (1 - core) * flip_y + core * flip_x
    chips = (near_a, near_b, me + 4, me - 4)
    sends = {plane: [] for plane in EVERY}

    def on(planes, act_on):
        for plane in planes:
            pl.when(z == plane)(functools.partial(act_on, plane))

    def remote(src, dst, send, recv, chip, on_core=None):
        return pltpu.make_async_remote_copy(
            src_ref=src, dst_ref=dst, send_sem=send, recv_sem=recv,
            device_id=(chip, core if on_core is None else on_core), device_id_type=MESH,
        )

    def arrived(ref, recv):
        remote(ref, ref, a_send.at[0, 0], recv, near_a).wait_recv()

    barrier = pltpu.get_barrier_semaphore()
    for peer in ((near_a, core), (near_b, core), (me, 1 - core)):
        pl.semaphore_signal(barrier, inc=1, device_id=peer, device_id_type=MESH)

    def greet(plane):
        for step, there in ((4, plane + 1), (-4, plane - 1)):
            if 0 <= there < LINE:
                pl.semaphore_signal(
                    barrier, inc=1, device_id=(me + step, core), device_id_type=MESH
                )
        pl.semaphore_wait(barrier, 4 if plane in ENDS else 5)

    on(EVERY, greet)

    def start(plane, copy):
        copy().start()
        sends[plane].append(copy)

    part_rows = rows // 2

    def piece(h):
        return pl.ds(h * part_rows, part_rows)

    def ship(plane, source, from_slot, to_slot, kind, h):
        start(plane, lambda: remote(
            source(), xs.at[to_slot, piece(h)], x_send.at[kind, from_slot, h],
            x_recv.at[to_slot, h], chips[kind]))

    def landed(slot, h):
        arrived(xs.at[slot, piece(h)], x_recv.at[slot, h])
        return lambda: xs.at[slot, piece(h)]

    def ship_along(plane, source, line, rank, h):
        there = NEAREST[plane][rank]
        slot = slot_of(line, rank)
        if plane < LINE - 1 and there <= plane:
            ship(plane, source, slot, slot_of(line, NEAREST[plane + 1].index(there)), TO_UP, h)
        if plane > 0 and there >= plane:
            ship(plane, source, slot, slot_of(line, NEAREST[plane - 1].index(there)), TO_DOWN, h)

    def own_piece(h):
        return ext_ref.at[piece(h)]

    def send_own(plane):
        for h in range(2):
            source = functools.partial(own_piece, h)
            ship(plane, source, 0, slot_of(SIDE_A, 0), TO_A, h)
            ship(plane, source, 0, slot_of(SIDE_B, 0), TO_B, h)
            ship_along(plane, source, OWN, 0, h)

    def relay_own(rank):
        def act_on(plane):
            slot = slot_of(OWN, rank)
            for h in range(2):
                source = landed(slot, h)
                ship_along(plane, source, OWN, rank, h)
                ship(plane, source, slot, slot_of(SIDE_A, rank), TO_A, h)
                ship(plane, source, slot, slot_of(SIDE_B, rank), TO_B, h)
        return act_on

    def relay_side(plane):
        slot = slot_of(SIDE_A, 0)
        for h in range(2):
            ship(plane, landed(slot, h), slot, slot_of(DIAGONAL, 0), TO_B, h)

    def relay_diagonal(rank):
        def act_on(plane):
            for h in range(2):
                ship_along(plane, landed(slot_of(DIAGONAL, rank), h), DIAGONAL, rank, h)
        return act_on

    def wait_for(line, rank):
        for h in range(2):
            landed(slot_of(line, rank), h)

    def stage_copy(ct):
        return pltpu.make_async_copy(
            w_in_ref.at[0, :, :, pl.ds(ct * LANES, LANES)], stage.at[ct % 2], w_sem.at[ct % 2]
        )

    def sort_tile(ct):
        stage_copy(ct).wait()
        at_cols = slice(ct * LANES, (ct + 1) * LANES)

        def body(k, carry):
            at = pl.ds(pl.multiple_of(k * LANES, LANES), LANES)
            wg[at, at_cols] = stage[ct % 2, at, 0, :]
            wu[at, at_cols] = stage[ct % 2, at, 1, :]
            return carry

        lax.fori_loop(0, cols // LANES, body, 0)
        if ct + 2 < hidden // LANES:
            stage_copy(ct + 2).start()

    def exchange(s, first_slot, count, j):
        at = pl.ds(first_slot * rows, count * rows)
        return remote(sent.at[j, :, at], got.at[j, :, at], p_send.at[s, j], p_recv.at[s, j],
                      me, 1 - core)

    def project_in(s, first_slot, count):
        size = count * rows
        block = pl.ds(first_slot, count)
        at_rows = pl.ds(first_slot * rows, size)

        def body(j, carry):
            at = pl.ds(pl.multiple_of(j * TILE, TILE), TILE)
            value = xs[block, :, :cols].reshape(size, cols)
            gate = jnp.dot(value, wg[:, at], preferred_element_type=jnp.float32)
            up = jnp.dot(value, wu[:, at], preferred_element_type=jnp.float32)
            part[j, 0, :size] = gate
            part[j, 1, :size] = up
            for k, value in ((0, gate), (1, up)):
                value = value.astype(jnp.bfloat16)
                if LINE <= first_slot < 3 * LINE:
                    sent[j, k, pl.ds(first_slot * rows, size // 2)] = value[size // 2:]
                    sent[j, k, pl.ds(first_slot * rows + size // 2, size // 2)] = value[:size // 2]
                else:
                    sent[j, k, at_rows] = value
            exchange(s, first_slot, count, j).start()
            return carry

        lax.fori_loop(0, tiles, body, 0)

    def activate(s, first_slot, count):
        size = count * rows
        at_rows = pl.ds(first_slot * rows, size)

        def body(j, carry):
            exchange(s, first_slot, count, j).wait_recv()
            gate = part[j, 0, :size] + got[j, 0, at_rows].astype(jnp.float32)
            up = part[j, 1, :size] + got[j, 1, at_rows].astype(jnp.float32)
            act[:size, pl.ds(pl.multiple_of(j * TILE, TILE), TILE)] = (
                gate / (1.0 + jnp.exp(-gate)) * up
            ).astype(jnp.bfloat16)
            return carry

        lax.fori_loop(0, tiles, body, 0)

    wide_tiles = cols // WIDE_TILE
    bounds = (0, (wide_tiles + 1) // 2, wide_tiles)

    def cut(h):
        return pl.ds(bounds[h] * WIDE_TILE, (bounds[h + 1] - bounds[h]) * WIDE_TILE)

    def project_out(first_slot, count, h):
        size = count * rows
        block = pl.ds(first_slot, count)
        lane = lax.broadcasted_iota(jnp.int32, (size, LANES), 1)
        mine = (lane % 16 == me) & (lane < 48)
        scales = xs[block, :, cols:].reshape(size, LANES).astype(jnp.float32)
        scale = jnp.sum(jnp.where(mine, scales, 0.0), axis=1, keepdims=True)

        def body(j, carry):
            at = pl.ds(pl.multiple_of(j * WIDE_TILE, WIDE_TILE), WIDE_TILE)
            value = jnp.dot(act[:size], wo[:, at], preferred_element_type=jnp.float32)
            value = value * scale
            contrib[block, :, at] = value.astype(jnp.bfloat16).reshape(count, rows, WIDE_TILE)
            return carry

        lax.fori_loop(bounds[h], bounds[h + 1], body, 0)

    def add_up(h, target, terms):
        def body(j, carry):
            at = pl.ds(pl.multiple_of(j * WIDE_TILE, WIDE_TILE), WIDE_TILE)
            total = terms[0][:, at].astype(jnp.float32)
            for term in terms[1:]:
                total = total + term[:, at].astype(jnp.float32)
            target[:, at] = total.astype(jnp.bfloat16)
            return carry

        lax.fori_loop(bounds[h], bounds[h + 1], body, 0)

    def pass_sum(plane, h, slot, target, send, recv, chip):
        start(plane, lambda: remote(
            contrib.at[slot, :, cut(h)], target[0].at[target[1]].at[:, cut(h)],
            send.at[(*target[1], h)], recv.at[(*target[1], h)], chip))

    def cross(rank, h):
        pass_sum("all", h, slot_of(SIDE_B, rank), (a_in, (rank,)), a_send, a_recv, near_a)
        pass_sum("all", h, slot_of(SIDE_A, rank), (b_in, (rank,)), b_send, b_recv, near_b)

    def straight(h):
        pass_sum("all", h, slot_of(SIDE_B, 0), (b_in, (0,)), b_send, b_recv, near_b)

    sends["all"] = []

    def take(buffer, recv, index, h):
        arrived(buffer.at[(*index, slice(None), cut(h))], recv.at[(*index, h)])
        return buffer.at[index]

    def along(line, rank, h):
        kind = line // DIAGONAL

        def act_on(plane):
            there = NEAREST[plane][rank]
            way = UP if there > plane else DOWN
            far = abs(there - plane)
            slot = slot_of(line, rank)
            terms = [contrib.at[slot]]
            if line == DIAGONAL:
                terms.append(take(a_in, a_recv, (rank,), h))
                terms.append(take(b_in, b_recv, (rank,), h))
            if plane != (0 if way == UP else LINE - 1):
                terms.append(take(z_in, z_recv, (kind, way, far), h))
            if len(terms) > 1:
                add_up(h, contrib.at[slot], terms)
            pass_sum(plane, h, slot, (z_in, (kind, way, far - 1)), z_send, z_recv,
                     chips[TO_UP if way == UP else TO_DOWN])
        return act_on

    def from_line(plane, kind, h):
        return [
            take(z_in, z_recv, (kind, way, 0), h)
            for way, stop in ((UP, 0), (DOWN, LINE - 1)) if plane != stop
        ]

    def turn_b(h):
        def act_on(plane):
            slot = slot_of(DIAGONAL, 0)
            add_up(h, contrib.at[slot], [contrib.at[slot], *from_line(plane, 1, h)])
            pass_sum(plane, h, slot, (b_in, (LINE,)), b_send, b_recv, near_b)
        return act_on

    def turn_a(h):
        slot = slot_of(SIDE_A, 0)
        add_up(h, contrib.at[slot], [contrib.at[slot], take(b_in, b_recv, (LINE,), h)])
        pass_sum("all", h, slot, (a_in, (0,)), a_send, a_recv, near_a)

    def finish(h):
        def act_on(plane):
            terms = [contrib.at[0], take(b_in, b_recv, (0,), h), *from_line(plane, 0, h)]
            add_up(h, out_ref, [*terms, take(a_in, a_recv, (0,), h)])
        return act_on

    groups = ((0, 2), (2, 2), (4, 4), (8, 4), (12, 2), (14, 2))

    def begin(s):
        project_in(s, *groups[s])
        activate(s, *groups[s])

    def close(s, h):
        project_out(*groups[s], h)

    on(EVERY, send_own)
    stage_copy(0).start()
    stage_copy(1).start()
    out_weights = pltpu.make_async_copy(w_out_ref.at[0], wo, wo_sem)
    out_weights.start()
    xs[0] = ext_ref[...]
    for ct in range(hidden // LANES):
        sort_tile(ct)
    on(EVERY, relay_side)
    on(EVERY, relay_own(1))
    on(INNER, relay_own(2))
    begin(0)
    out_weights.wait()
    close(0, 0)
    close(0, 1)
    on(INNER, relay_own(3))
    on(ENDS, relay_own(2))
    on(EVERY, relay_diagonal(0))
    for h in range(2):
        on(ENDS, along(OWN, 1, h))
    on(ENDS, relay_own(3))
    begin(1)
    for h in range(2):
        close(1, h)
        on(ENDS, along(OWN, 3, h))
        on(ENDS, along(OWN, 2, h))
    on(INNER, relay_diagonal(1))
    on(INNER, relay_diagonal(2))
    for rank in range(2):
        if rank:
            wait_for(SIDE_A, rank)
        wait_for(SIDE_B, rank)
    begin(2)
    on(INNER, relay_diagonal(3))
    for h in range(2):
        close(2, h)
        cross(1, h)
    for h in range(2):
        on(INNER, along(OWN, 3, h))
    for rank in (2, 3):
        wait_for(SIDE_A, rank)
        wait_for(SIDE_B, rank)
    begin(3)
    for h in range(2):
        close(3, h)
        cross(3, h)
        cross(2, h)
    for h in range(2):
        on(INNER, along(OWN, 2, h))
    on(ENDS, lambda plane: wait_for(DIAGONAL, 1))
    begin(4)
    for h in range(2):
        close(4, h)
        straight(h)
        on(ENDS, along(DIAGONAL, 1, h))
    for h in range(2):
        on(INNER, along(OWN, 1, h))
    on(ENDS, lambda plane: wait_for(DIAGONAL, 2))
    on(ENDS, lambda plane: wait_for(DIAGONAL, 3))
    begin(5)
    for h in range(2):
        close(5, h)
        on(ENDS, along(DIAGONAL, 3, h))
        on(ENDS, along(DIAGONAL, 2, h))
    for h in range(2):
        on(INNER, along(DIAGONAL, 3, h))
    for h in range(2):
        on(INNER, along(DIAGONAL, 2, h))
    for h in range(2):
        on(INNER, along(DIAGONAL, 1, h))
    for h in range(2):
        on(EVERY, turn_b(h))
    for h in range(2):
        turn_a(h)
    for h in range(2):
        on(EVERY, finish(h))
    for copy in sends["all"]:
        copy().wait_send()

    def drained(plane):
        for copy in sends[plane]:
            copy().wait_send()

    on(EVERY, drained)
    for s, (first_slot, count) in enumerate(groups):
        def drain(j, carry):
            exchange(s, first_slot, count, j).wait_send()
            return carry

        lax.fori_loop(0, tiles, drain, 0)


def fused(tokens, routes, route_scores, placement, w_in, w_out):
    rows, cols = tokens.shape
    hidden = w_in.shape[3]
    tiles = hidden // TILE
    table = expert_weights(routes, route_scores, placement)
    high = lax.reduce_precision(table, 8, 7)
    middle = lax.reduce_precision(table - high, 8, 7)
    low = table - high - middle
    thirds = [third.astype(jnp.bfloat16) for third in (high, middle, low)]
    filler = jnp.zeros((rows, LANES - 3 * table.shape[1]), jnp.bfloat16)
    ext = jnp.concatenate([tokens, *thirds, filler], axis=1)
    slots = LINE * LINE
    bf16 = jnp.bfloat16
    dma = pltpu.SemaphoreType.DMA
    return pl.pallas_call(
        layer_kernel,
        out_shape=jax.ShapeDtypeStruct((rows, cols), bf16),
        in_specs=[
            pl.BlockSpec(memory_space=pltpu.VMEM),
            pl.BlockSpec(memory_space=pl.ANY),
            pl.BlockSpec(memory_space=pl.ANY),
        ],
        out_specs=pl.BlockSpec(memory_space=pltpu.VMEM),
        scratch_shapes=[
            pltpu.VMEM((slots, rows, cols + LANES), bf16),
            pltpu.VMEM((cols, hidden), bf16),
            pltpu.VMEM((cols, hidden), bf16),
            pltpu.VMEM((2, cols, 2, LANES), bf16),
            pltpu.VMEM((hidden, cols), bf16),
            pltpu.VMEM((slots, rows, cols), bf16),
            pltpu.VMEM((2, 2, LINE - 1, rows, cols), bf16),
            pltpu.VMEM((LINE, rows, cols), bf16),
            pltpu.VMEM((LINE + 1, rows, cols), bf16),
            pltpu.VMEM((tiles, 2, LINE * rows, TILE), jnp.float32),
            pltpu.VMEM((tiles, 2, slots * rows, TILE), bf16),
            pltpu.VMEM((tiles, 2, slots * rows, TILE), bf16),
            pltpu.VMEM((LINE * rows, hidden), bf16),
            dma((2,)), dma, dma((4, slots, 2)), dma((slots, 2)),
            dma((slots, tiles)), dma((slots, tiles)),
            dma((2, 2, LINE - 1, 2)), dma((2, 2, LINE - 1, 2)),
            dma((LINE, 2)), dma((LINE, 2)), dma((LINE + 1, 2)), dma((LINE + 1, 2)),
        ],
        compiler_params=pltpu.CompilerParams(
            collective_id=0, has_side_effects=True, vmem_limit_bytes=67043328
        ),
    )(ext, w_in, w_out)


def on_device(tokens, routes, route_scores, placement, w_in, w_out):
    tok_rows = tokens.shape[0]
    experts = placement.shape[0]
    fits = experts == 4 * LINE and lax.axis_size("replica") == 2
    if fits and 2 * tok_rows * routes.shape[1] // experts >= tok_rows:
        return fused(tokens, routes, route_scores, placement, w_in, w_out)
    return packed(tokens, routes, route_scores, placement, w_in, w_out)


def solution(mesh):
    in_specs = (
        P("expert", "replica"),
        P("expert", None),
        P("expert", None),
        P(),
        P("expert", "replica", None, None),
        P("expert", None, "replica"),
    )
    out_specs = P("expert", "replica")
    return jax.shard_map(
        on_device, mesh=mesh, in_specs=in_specs, out_specs=out_specs, check_vma=False
    )
```

time: 193 us -> 170 us (0.88)
  Pallas kernels: 183 us -> 161 us
    pallas_call x1, Pallas kernels: 183 us -> 161 us  [fused(): pl.pallas_call(layer_kernel, out_shape=jax.ShapeDtypeStruct((rows, cols),...]
where the time goes in v2:
time: 170 us; the launch traced here: 167 us
  Pallas kernels  161 us (95%)
  local copies, waits for them, and re-layouts  3.87 us (2%)
  other arithmetic  2.22 us (1%)
    pallas_call x1, Pallas kernels, fused(): pl.pallas_call(layer_kernel, out_shape=jax.ShapeDtypeStruct((rows, cols),...  161 us

profile of v2, /device:TPU:8, one launch (start us, length us, event | category | flops | bytes accessed | tf_op | source)
XLA Modules:
  0.0 167.2 jit_solution(12857390678465134247)
XLA Ops:
  0.0 0.7 reduce_sum.28
  0.7 0.7 multiply_divide_fusion
  1.4 0.8 select_reduce_fusion.1
  2.2 0.1 copy.12
  2.3 0.1 copy.11
  2.4 1.9 %concatenate.3.ext_ref = bf16[64,3712]{1,0:T(8,128)(2,1)} concatenate(bf16[64,3584]{1,0:T(8,128)(2,1)} %param.6, bf16[64,16]{1,0:T(8,128)(2,1)S(1)} %get-tuple-element.7, bf16[64,16]{1,0:T(8,128)(2,1)S(1)} %get-tuple-element.6, bf16[64,16]{1,0:T(8,128)(2,1)S(1)} %get-tuple-element.5, bf16[64,80]{1,0:T(8,128)(2,1)S(1)} %broadcast_in_dim.33), dimensions={1} | concatenate | bytes 950272 | tf_op jit(solution)/shard_map/concatenate | solution.py:456
  4.3 161.0 %shard_map.64 = bf16[64,3584]{1,0:T(8,128)(2,1)} custom-call(bf16[64,3712]{1,0:T(8,128)(2,1)} %concatenate.3.ext_ref, bf16[1,3584,2,1024]{3,2,1,0:T(2,128)(2,1)} %w_in_ref.1, bf16[1,1024,3584]{2,1,0:T(8,128)(2,1)} %w_out_ref.1), custom_call_target="tpu_custom_call" | custom-call | tf_op jit(solution)/shard_map/pallas_call | solution.py:460
  165.3 1.8 %copy.15 = bf16[64,3584]{1,0:T(8,128)(2,1)} copy(bf16[64,3584]{1,0:T(8,128)(2,1)} %shard_map.64) | data formatting | bytes 917504
  (4 shorter events, 0.0 us)

commit v3 on v2

--- a/solution.py
+++ b/solution.py
@@ -10,6 +10,7 @@
 LANES = 128
 TILE = 256
 WIDE_TILE = 512
+PIECES = 4
 MESH = pl.DeviceIdType.MESH
 LINE = 4
 OWN, SIDE_A, SIDE_B, DIAGONAL = range(4)
@@ -17,14 +18,20 @@
 TO_A, TO_B, TO_UP, TO_DOWN = range(4)
 NEAREST = ((0, 1, 2, 3), (1, 0, 2, 3), (2, 3, 1, 0), (3, 2, 1, 0))
 ENDS, INNER, EVERY = (0, LINE - 1), (1, 2), (0, 1, 2, 3)
+SLOTS = (
+    (OWN, 0), (OWN, 1), (SIDE_A, 0), (SIDE_B, 0), (OWN, 2), (OWN, 3), (SIDE_A, 1), (SIDE_B, 1),
+    (SIDE_A, 2), (SIDE_B, 2), (SIDE_A, 3), (SIDE_B, 3),
+    (DIAGONAL, 0), (DIAGONAL, 1), (DIAGONAL, 2), (DIAGONAL, 3),
+)
 
 
 def slot_of(line, rank):
-    if line == OWN:
-        return rank
-    if line == DIAGONAL:
-        return 3 * LINE + rank
-    return LINE * (1 + rank // 2) + 2 * (line - 1) + rank % 2
+    return SLOTS.index((line, rank))
+
+
+def twin_of(slot):
+    line, rank = SLOTS[slot]
+    return slot_of({SIDE_A: SIDE_B, SIDE_B: SIDE_A}.get(line, line), rank)
 
 
 def packed(tokens, routes, route_scores, placement, w_in, w_out):
@@ -78,7 +85,7 @@
 
 def layer_kernel(
     ext_ref, w_in_ref, w_out_ref, out_ref,
-    xs, wg, wu, stage, wo, contrib, z_in, a_in, b_in, part, sent, got, act,
+    xs, wg, wu, stage, pairs, wo, contrib, z_in, a_in, b_in, part, sent, got, act,
     w_sem, wo_sem, x_send, x_recv, p_send, p_recv,
     z_send, z_recv, a_send, a_recv, b_send, b_recv,
 ):
@@ -158,25 +165,40 @@
             ship(plane, source, 0, slot_of(SIDE_B, 0), TO_B, h)
             ship_along(plane, source, OWN, 0, h)
 
-    def relay_own(rank):
+    def relay_own(rank, h):
         def act_on(plane):
             slot = slot_of(OWN, rank)
-            for h in range(2):
-                source = landed(slot, h)
-                ship_along(plane, source, OWN, rank, h)
-                ship(plane, source, slot, slot_of(SIDE_A, rank), TO_A, h)
-                ship(plane, source, slot, slot_of(SIDE_B, rank), TO_B, h)
-        return act_on
-
-    def relay_side(plane):
-        slot = slot_of(SIDE_A, 0)
-        for h in range(2):
+            source = landed(slot, h)
+            ship_along(plane, source, OWN, rank, h)
+            ship(plane, source, slot, slot_of(SIDE_A, rank), TO_A, h)
+            ship(plane, source, slot, slot_of(SIDE_B, rank), TO_B, h)
+        return act_on
+
+    def pass_z(rank, h):
+        def act_on(plane):
+            ship_along(plane, landed(slot_of(OWN, rank), h), OWN, rank, h)
+        return act_on
+
+    def pass_ab(rank, h):
+        def act_on(plane):
+            slot = slot_of(OWN, rank)
+
+            def held():
+                return xs.at[slot, piece(h)]
+
+            ship(plane, held, slot, slot_of(SIDE_A, rank), TO_A, h)
+            ship(plane, held, slot, slot_of(SIDE_B, rank), TO_B, h)
+        return act_on
+
+    def relay_side(h):
+        def act_on(plane):
+            slot = slot_of(SIDE_A, 0)
             ship(plane, landed(slot, h), slot, slot_of(DIAGONAL, 0), TO_B, h)
-
-    def relay_diagonal(rank):
-        def act_on(plane):
-            for h in range(2):
-                ship_along(plane, landed(slot_of(DIAGONAL, rank), h), DIAGONAL, rank, h)
+        return act_on
+
+    def relay_diagonal(rank, h):
+        def act_on(plane):
+            ship_along(plane, landed(slot_of(DIAGONAL, rank), h), DIAGONAL, rank, h)
         return act_on
 
     def wait_for(line, rank):
@@ -192,13 +214,18 @@
         stage_copy(ct).wait()
         at_cols = slice(ct * LANES, (ct + 1) * LANES)
 
+        flat = stage.at[ct % 2].reshape(2 * cols, LANES)
+
         def body(k, carry):
-            at = pl.ds(pl.multiple_of(k * LANES, LANES), LANES)
-            wg[at, at_cols] = stage[ct % 2, at, 0, :]
-            wu[at, at_cols] = stage[ct % 2, at, 1, :]
+            for n in range(2):
+                first = pl.multiple_of((2 * k + n) * LANES, LANES)
+                at = pl.ds(first, LANES)
+                pairs[n] = flat[pl.ds(2 * first, 2 * LANES), :].astype(jnp.float32)
+                wg[at, at_cols] = pairs[n, pl.ds(0, LANES, stride=2), :].astype(jnp.bfloat16)
+                wu[at, at_cols] = pairs[n, pl.ds(1, LANES, stride=2), :].astype(jnp.bfloat16)
             return carry
 
-        lax.fori_loop(0, cols // LANES, body, 0)
+        lax.fori_loop(0, cols // (2 * LANES), body, 0)
         if ct + 2 < hidden // LANES:
             stage_copy(ct + 2).start()
 
@@ -221,11 +248,9 @@
             part[j, 1, :size] = up
             for k, value in ((0, gate), (1, up)):
                 value = value.astype(jnp.bfloat16)
-                if LINE <= first_slot < 3 * LINE:
-                    sent[j, k, pl.ds(first_slot * rows, size // 2)] = value[size // 2:]
-                    sent[j, k, pl.ds(first_slot * rows + size // 2, size // 2)] = value[:size // 2]
-                else:
-                    sent[j, k, at_rows] = value
+                for n in range(count):
+                    theirs = pl.ds(twin_of(first_slot + n) * rows, rows)
+                    sent[j, k, theirs] = value[n * rows:(n + 1) * rows]
             exchange(s, first_slot, count, j).start()
             return carry
 
@@ -247,7 +272,9 @@
         lax.fori_loop(0, tiles, body, 0)
 
     wide_tiles = cols // WIDE_TILE
-    bounds = (0, (wide_tiles + 1) // 2, wide_tiles)
+    per_piece = -(-wide_tiles // PIECES)
+    bounds = [min(n * per_piece, wide_tiles) for n in range(PIECES + 1)]
+    every_piece = [h for h in range(PIECES) if bounds[h] < bounds[h + 1]]
 
     def cut(h):
         return pl.ds(bounds[h] * WIDE_TILE, (bounds[h + 1] - bounds[h]) * WIDE_TILE)
@@ -342,90 +369,117 @@
             add_up(h, out_ref, [*terms, take(a_in, a_recv, (0,), h)])
         return act_on
 
-    groups = ((0, 2), (2, 2), (4, 4), (8, 4), (12, 2), (14, 2))
-
-    def begin(s):
+    def feed(s):
         project_in(s, *groups[s])
+
+    def blend(s):
         activate(s, *groups[s])
 
     def close(s, h):
         project_out(*groups[s], h)
 
     on(EVERY, send_own)
+    tiles_in = hidden // LANES
     stage_copy(0).start()
     stage_copy(1).start()
     out_weights = pltpu.make_async_copy(w_out_ref.at[0], wo, wo_sem)
     out_weights.start()
     xs[0] = ext_ref[...]
-    for ct in range(hidden // LANES):
+    groups = ((0, 2), (2, 2), (4, 4), (8, 2), (10, 2), (12, 4))
+    for ct in range(tiles_in // 2):
         sort_tile(ct)
-    on(EVERY, relay_side)
-    on(EVERY, relay_own(1))
-    on(INNER, relay_own(2))
-    begin(0)
+    on(EVERY, relay_side(0))
+    on(EVERY, pass_z(1, 0))
+    on(INNER, pass_z(2, 0))
+    for ct in range(tiles_in // 2, tiles_in):
+        sort_tile(ct)
+    on(EVERY, relay_side(1))
+    on(EVERY, pass_z(1, 1))
+    on(EVERY, pass_ab(1, 0))
+    on(EVERY, pass_ab(1, 1))
+    on(INNER, pass_z(2, 1))
+    on(INNER, pass_ab(2, 0))
+    on(INNER, pass_ab(2, 1))
+    feed(0)
+    on(INNER, pass_z(3, 0))
+    on(ENDS, relay_own(2, 0))
+    on(EVERY, relay_diagonal(0, 0))
+    blend(0)
     out_weights.wait()
-    close(0, 0)
-    close(0, 1)
-    on(INNER, relay_own(3))
-    on(ENDS, relay_own(2))
-    on(EVERY, relay_diagonal(0))
-    for h in range(2):
+    for h in every_piece:
+        close(0, h)
+    on(INNER, pass_z(3, 1))
+    on(INNER, pass_ab(3, 0))
+    on(INNER, pass_ab(3, 1))
+    on(ENDS, relay_own(2, 1))
+    on(EVERY, relay_diagonal(0, 1))
+    for h in every_piece:
         on(ENDS, along(OWN, 1, h))
-    on(ENDS, relay_own(3))
-    begin(1)
-    for h in range(2):
+    wait_for(SIDE_B, 0)
+    feed(1)
+    on(INNER, relay_diagonal(1, 0))
+    on(ENDS, relay_own(3, 0))
+    blend(1)
+    for h in every_piece:
         close(1, h)
+        straight(h)
+    on(ENDS, relay_own(3, 1))
+    on(INNER, relay_diagonal(1, 1))
+    on(INNER, relay_diagonal(2, 0))
+    wait_for(SIDE_A, 1)
+    wait_for(SIDE_B, 1)
+    feed(2)
+    on(INNER, relay_diagonal(2, 1))
+    on(INNER, relay_diagonal(3, 0))
+    blend(2)
+    for h in every_piece:
+        close(2, h)
+        cross(1, h)
         on(ENDS, along(OWN, 3, h))
         on(ENDS, along(OWN, 2, h))
-    on(INNER, relay_diagonal(1))
-    on(INNER, relay_diagonal(2))
-    for rank in range(2):
-        if rank:
-            wait_for(SIDE_A, rank)
-        wait_for(SIDE_B, rank)
-    begin(2)
-    on(INNER, relay_diagonal(3))
-    for h in range(2):
-        close(2, h)
-        cross(1, h)
-    for h in range(2):
+    on(INNER, relay_diagonal(3, 1))
+    wait_for(SIDE_A, 2)
+    wait_for(SIDE_B, 2)
+    feed(3)
+    blend(3)
+    for h in every_piece:
+        close(3, h)
+    wait_for(SIDE_A, 3)
+    wait_for(SIDE_B, 3)
+    feed(4)
+    for h in every_piece[:PIECES // 2]:
         on(INNER, along(OWN, 3, h))
-    for rank in (2, 3):
-        wait_for(SIDE_A, rank)
-        wait_for(SIDE_B, rank)
-    begin(3)
-    for h in range(2):
-        close(3, h)
+    blend(4)
+    for h in every_piece[PIECES // 2:]:
+        on(INNER, along(OWN, 3, h))
+    for h in every_piece:
+        close(4, h)
         cross(3, h)
+    for h in every_piece:
         cross(2, h)
-    for h in range(2):
+    for rank in (1, 2, 3):
+        on(ENDS, lambda plane: wait_for(DIAGONAL, rank))
+    feed(5)
+    for h in every_piece:
         on(INNER, along(OWN, 2, h))
-    on(ENDS, lambda plane: wait_for(DIAGONAL, 1))
-    begin(4)
-    for h in range(2):
-        close(4, h)
-        straight(h)
-        on(ENDS, along(DIAGONAL, 1, h))
-    for h in range(2):
         on(INNER, along(OWN, 1, h))
-    on(ENDS, lambda plane: wait_for(DIAGONAL, 2))
-    on(ENDS, lambda plane: wait_for(DIAGONAL, 3))
-    begin(5)
-    for h in range(2):
+    blend(5)
+    for h in every_piece:
         close(5, h)
         on(ENDS, along(DIAGONAL, 3, h))
+    for h in every_piece:
+        on(INNER, along(DIAGONAL, 3, h))
+    for h in every_piece:
         on(ENDS, along(DIAGONAL, 2, h))
-    for h in range(2):
-        on(INNER, along(DIAGONAL, 3, h))
-    for h in range(2):
+        on(INNER, along(DIAGONAL, 1, h))
+    for h in every_piece:
+        on(ENDS, along(DIAGONAL, 1, h))
         on(INNER, along(DIAGONAL, 2, h))
-    for h in range(2):
-        on(INNER, along(DIAGONAL, 1, h))
-    for h in range(2):
+    for h in every_piece:
         on(EVERY, turn_b(h))
-    for h in range(2):
+    for h in every_piece:
         turn_a(h)
-    for h in range(2):
+    for h in every_piece:
         on(EVERY, finish(h))
     for copy in sends["all"]:
         copy().wait_send()
@@ -471,6 +525,7 @@
             pltpu.VMEM((cols, hidden), bf16),
             pltpu.VMEM((cols, hidden), bf16),
             pltpu.VMEM((2, cols, 2, LANES), bf16),
+            pltpu.VMEM((2, 2 * LANES, LANES), jnp.float32),
             pltpu.VMEM((hidden, cols), bf16),
             pltpu.VMEM((slots, rows, cols), bf16),
             pltpu.VMEM((2, 2, LINE - 1, rows, cols), bf16),
@@ -482,8 +537,9 @@
             pltpu.VMEM((LINE * rows, hidden), bf16),
             dma((2,)), dma, dma((4, slots, 2)), dma((slots, 2)),
             dma((slots, tiles)), dma((slots, tiles)),
-            dma((2, 2, LINE - 1, 2)), dma((2, 2, LINE - 1, 2)),
-            dma((LINE, 2)), dma((LINE, 2)), dma((LINE + 1, 2)), dma((LINE + 1, 2)),
+            dma((2, 2, LINE - 1, PIECES)), dma((2, 2, LINE - 1, PIECES)),
+            dma((LINE, PIECES)), dma((LINE, PIECES)),
+            dma((LINE + 1, PIECES)), dma((LINE + 1, PIECES)),
         ],
         compiler_params=pltpu.CompilerParams(
             collective_id=0, has_side_effects=True, vmem_limit_bytes=67043328

time: 170 us -> 131 us (0.77); the launches traced: 167 us -> 130 us
  Pallas kernels: 161 us -> 124 us
    pallas_call x1, Pallas kernels: 161 us -> 124 us  [fused(): pl.pallas_call(layer_kernel, out_shape=jax.ShapeDtypeStruct((rows, cols),...]
where the time goes in v3:
time: 131 us; the launch traced here: 130 us
  Pallas kernels  124 us (95%)
  local copies, waits for them, and re-layouts  3.87 us (3%)
  other arithmetic  2.22 us (2%)
    pallas_call x1, Pallas kernels, fused(): pl.pallas_call(layer_kernel, out_shape=jax.ShapeDtypeStruct((rows, cols),...  124 us

profile of v3, /device:TPU:8, one launch (start us, length us, event | category | flops | bytes accessed | tf_op | source)
XLA Modules:
  0.0 130.3 jit_solution(7780542032791857230)
XLA Ops:
  0.0 0.7 reduce_sum.28
  0.7 0.7 multiply_divide_fusion
  1.4 0.8 select_reduce_fusion.1
  2.2 0.1 copy.12
  2.3 0.1 copy.11
  2.4 1.9 %concatenate.3.ext_ref = bf16[64,3712]{1,0:T(8,128)(2,1)} concatenate(bf16[64,3584]{1,0:T(8,128)(2,1)} %param.6, bf16[64,16]{1,0:T(8,128)(2,1)S(1)} %get-tuple-element.7, bf16[64,16]{1,0:T(8,128)(2,1)S(1)} %get-tuple-element.6, bf16[64,16]{1,0:T(8,128)(2,1)S(1)} %get-tuple-element.5, bf16[64,80]{1,0:T(8,128)(2,1)S(1)} %broadcast_in_dim.33), dimensions={1} | concatenate | bytes 950272 | tf_op jit(solution)/shard_map/concatenate | solution.py:510
  4.3 124.2 %shard_map.64 = bf16[64,3584]{1,0:T(8,128)(2,1)} custom-call(bf16[64,3712]{1,0:T(8,128)(2,1)} %concatenate.3.ext_ref, bf16[1,3584,2,1024]{3,2,1,0:T(2,128)(2,1)} %w_in_ref.1, bf16[1,1024,3584]{2,1,0:T(8,128)(2,1)} %w_out_ref.1), custom_call_target="tpu_custom_call" | custom-call | tf_op jit(solution)/shard_map/pallas_call | solution.py:514
  128.5 1.8 %copy.15 = bf16[64,3584]{1,0:T(8,128)(2,1)} copy(bf16[64,3584]{1,0:T(8,128)(2,1)} %shard_map.64) | data formatting | bytes 917504
  (4 shorter events, 0.0 us)

commit v4 on v3

--- a/solution.py
+++ b/solution.py
@@ -11,6 +11,7 @@
 TILE = 256
 WIDE_TILE = 512
 PIECES = 4
+DEPTH = 3
 MESH = pl.DeviceIdType.MESH
 LINE = 4
 OWN, SIDE_A, SIDE_B, DIAGONAL = range(4)
@@ -73,25 +74,47 @@
     return mixed.astype(jnp.bfloat16)
 
 
-def expert_weights(routes, route_scores, placement):
-    experts = placement.shape[0]
-    expert_ids = jnp.arange(experts, dtype=jnp.int32)
-    physical = jnp.sum(jnp.where(routes[:, :, None] == expert_ids, placement, 0), axis=-1)
-    route_weight = 2.5 * route_scores / jnp.sum(route_scores, axis=1, keepdims=True)
-    return jnp.sum(
-        jnp.where(physical[:, :, None] == expert_ids, route_weight[:, :, None], 0.0), axis=1
-    )
+def weight_columns(routes_ref, scores_ref, placement_ref):
+    routes = routes_ref[...]
+    scores = scores_ref[...]
+    experts = placement_ref.shape[0]
+    physical = jnp.zeros_like(routes)
+    for expert in range(experts):
+        physical = jnp.where(routes == expert, placement_ref[expert], physical)
+    route_weight = 2.5 * scores / jnp.sum(scores, axis=0, keepdims=True)
+    column = lax.broadcasted_iota(jnp.int32, (LANES, routes.shape[1]), 0)
+    table = jnp.zeros(column.shape, jnp.float32)
+    for k in range(routes.shape[0]):
+        chosen = physical[k:k + 1, :] == column % experts
+        table = jnp.where(chosen, route_weight[k:k + 1, :], table)
+    high = table.astype(jnp.bfloat16).astype(jnp.float32)
+    middle = (table - high).astype(jnp.bfloat16).astype(jnp.float32)
+    low = table - high - middle
+    thirds = jnp.where(column < experts, high, jnp.where(column < 2 * experts, middle, low))
+    return jnp.where(column < 3 * experts, thirds, 0.0).T.astype(jnp.bfloat16)
 
 
 def layer_kernel(
-    ext_ref, w_in_ref, w_out_ref, out_ref,
+    tokens_ref, routes_ref, scores_ref, placement_ref, w_in_ref, w_out_ref, out_ref,
     xs, wg, wu, stage, pairs, wo, contrib, z_in, a_in, b_in, part, sent, got, act,
-    w_sem, wo_sem, x_send, x_recv, p_send, p_recv,
+    t_sem, w_sem, wo_sem, x_send, x_recv, p_send, p_recv,
     z_send, z_recv, a_send, a_recv, b_send, b_recv,
 ):
-    rows, width = ext_ref.shape
-    cols = out_ref.shape[1]
+    rows, cols = out_ref.shape
     hidden = wg.shape[1]
+    own_tokens = pltpu.make_async_copy(tokens_ref, xs.at[0, :, :cols], t_sem)
+    own_tokens.start()
+    out_weights = pltpu.make_async_copy(w_out_ref.at[0], wo, wo_sem)
+
+    def stage_copy(ct):
+        return pltpu.make_async_copy(
+            w_in_ref.at[0].reshape(2 * cols, hidden).at[:, pl.ds(ct * LANES, LANES)],
+            stage.at[ct % DEPTH], w_sem.at[ct % DEPTH]
+        )
+
+    for ct in range(DEPTH):
+        stage_copy(ct).start()
+    xs[0, :, cols:] = weight_columns(routes_ref, scores_ref, placement_ref)
     tiles = hidden // TILE
     me = lax.axis_index("expert")
     core = lax.axis_index("replica")
@@ -156,7 +179,7 @@
             ship(plane, source, slot, slot_of(line, NEAREST[plane - 1].index(there)), TO_DOWN, h)
 
     def own_piece(h):
-        return ext_ref.at[piece(h)]
+        return xs.at[0, piece(h)]
 
     def send_own(plane):
         for h in range(2):
@@ -205,16 +228,11 @@
         for h in range(2):
             landed(slot_of(line, rank), h)
 
-    def stage_copy(ct):
-        return pltpu.make_async_copy(
-            w_in_ref.at[0, :, :, pl.ds(ct * LANES, LANES)], stage.at[ct % 2], w_sem.at[ct % 2]
-        )
-
     def sort_tile(ct):
         stage_copy(ct).wait()
         at_cols = slice(ct * LANES, (ct + 1) * LANES)
 
-        flat = stage.at[ct % 2].reshape(2 * cols, LANES)
+        flat = stage.at[ct % DEPTH]
 
         def body(k, carry):
             for n in range(2):
@@ -226,50 +244,36 @@
             return carry
 
         lax.fori_loop(0, cols // (2 * LANES), body, 0)
-        if ct + 2 < hidden // LANES:
-            stage_copy(ct + 2).start()
+        if ct + DEPTH < hidden // LANES:
+            stage_copy(ct + DEPTH).start()
+        if ct + DEPTH == hidden // LANES:
+            out_weights.start()
 
     def exchange(s, first_slot, count, j):
         at = pl.ds(first_slot * rows, count * rows)
         return remote(sent.at[j, :, at], got.at[j, :, at], p_send.at[s, j], p_recv.at[s, j],
                       me, 1 - core)
 
-    def project_in(s, first_slot, count):
+    def project_in(s, first_slot, count, j):
         size = count * rows
-        block = pl.ds(first_slot, count)
-        at_rows = pl.ds(first_slot * rows, size)
-
-        def body(j, carry):
-            at = pl.ds(pl.multiple_of(j * TILE, TILE), TILE)
-            value = xs[block, :, :cols].reshape(size, cols)
-            gate = jnp.dot(value, wg[:, at], preferred_element_type=jnp.float32)
-            up = jnp.dot(value, wu[:, at], preferred_element_type=jnp.float32)
-            part[j, 0, :size] = gate
-            part[j, 1, :size] = up
-            for k, value in ((0, gate), (1, up)):
-                value = value.astype(jnp.bfloat16)
-                for n in range(count):
-                    theirs = pl.ds(twin_of(first_slot + n) * rows, rows)
-                    sent[j, k, theirs] = value[n * rows:(n + 1) * rows]
-            exchange(s, first_slot, count, j).start()
-            return carry
-
-        lax.fori_loop(0, tiles, body, 0)
-
-    def activate(s, first_slot, count):
+        at = pl.ds(j * TILE if isinstance(j, int) else pl.multiple_of(j * TILE, TILE), TILE)
+        value = xs[pl.ds(first_slot, count), :, :cols].reshape(size, cols)
+        for k, weights in ((0, wg), (1, wu)):
+            total = jnp.dot(value, weights[:, at], preferred_element_type=jnp.float32)
+            part[j, k, :size] = total
+            total = total.astype(jnp.bfloat16)
+            for n in range(count):
+                theirs = pl.ds(twin_of(first_slot + n) * rows, rows)
+                sent[j, k, theirs] = total[n * rows:(n + 1) * rows]
+        exchange(s, first_slot, count, j).start()
+
+    def activate(first_slot, count, j):
         size = count * rows
         at_rows = pl.ds(first_slot * rows, size)
-
-        def body(j, carry):
-            exchange(s, first_slot, count, j).wait_recv()
-            gate = part[j, 0, :size] + got[j, 0, at_rows].astype(jnp.float32)
-            up = part[j, 1, :size] + got[j, 1, at_rows].astype(jnp.float32)
-            act[:size, pl.ds(pl.multiple_of(j * TILE, TILE), TILE)] = (
-                gate / (1.0 + jnp.exp(-gate)) * up
-            ).astype(jnp.bfloat16)
-            return carry
-
-        lax.fori_loop(0, tiles, body, 0)
+        gate = part[j, 0, :size] + got[j, 0, at_rows].astype(jnp.float32)
+        up = part[j, 1, :size] + got[j, 1, at_rows].astype(jnp.float32)
+        at = pl.ds(j * TILE if isinstance(j, int) else pl.multiple_of(j * TILE, TILE), TILE)
+        act[:size, at] = (gate / (1.0 + jnp.exp(-gate)) * up).astype(jnp.bfloat16)
 
     wide_tiles = cols // WIDE_TILE
     per_piece = -(-wide_tiles // PIECES)
@@ -370,21 +374,26 @@
         return act_on
 
     def feed(s):
-        project_in(s, *groups[s])
+        def body(j, carry):
+            project_in(s, *groups[s], j)
+            return carry
+
+        lax.fori_loop(0, tiles, body, 0)
 
     def blend(s):
-        activate(s, *groups[s])
+        def body(j, carry):
+            exchange(s, *groups[s], j).wait_recv()
+            activate(*groups[s], j)
+            return carry
+
+        lax.fori_loop(0, tiles, body, 0)
 
     def close(s, h):
         project_out(*groups[s], h)
 
+    own_tokens.wait()
     on(EVERY, send_own)
     tiles_in = hidden // LANES
-    stage_copy(0).start()
-    stage_copy(1).start()
-    out_weights = pltpu.make_async_copy(w_out_ref.at[0], wo, wo_sem)
-    out_weights.start()
-    xs[0] = ext_ref[...]
     groups = ((0, 2), (2, 2), (4, 4), (8, 2), (10, 2), (12, 4))
     for ct in range(tiles_in // 2):
         sort_tile(ct)
@@ -501,13 +510,6 @@
     rows, cols = tokens.shape
     hidden = w_in.shape[3]
     tiles = hidden // TILE
-    table = expert_weights(routes, route_scores, placement)
-    high = lax.reduce_precision(table, 8, 7)
-    middle = lax.reduce_precision(table - high, 8, 7)
-    low = table - high - middle
-    thirds = [third.astype(jnp.bfloat16) for third in (high, middle, low)]
-    filler = jnp.zeros((rows, LANES - 3 * table.shape[1]), jnp.bfloat16)
-    ext = jnp.concatenate([tokens, *thirds, filler], axis=1)
     slots = LINE * LINE
     bf16 = jnp.bfloat16
     dma = pltpu.SemaphoreType.DMA
@@ -515,7 +517,10 @@
         layer_kernel,
         out_shape=jax.ShapeDtypeStruct((rows, cols), bf16),
         in_specs=[
+            pl.BlockSpec(memory_space=pl.ANY),
             pl.BlockSpec(memory_space=pltpu.VMEM),
+            pl.BlockSpec(memory_space=pltpu.VMEM),
+            pl.BlockSpec(memory_space=pltpu.SMEM),
             pl.BlockSpec(memory_space=pl.ANY),
             pl.BlockSpec(memory_space=pl.ANY),
         ],
@@ -524,7 +529,7 @@
             pltpu.VMEM((slots, rows, cols + LANES), bf16),
             pltpu.VMEM((cols, hidden), bf16),
             pltpu.VMEM((cols, hidden), bf16),
-            pltpu.VMEM((2, cols, 2, LANES), bf16),
+            pltpu.VMEM((DEPTH, 2 * cols, LANES), bf16),
             pltpu.VMEM((2, 2 * LANES, LANES), jnp.float32),
             pltpu.VMEM((hidden, cols), bf16),
             pltpu.VMEM((slots, rows, cols), bf16),
@@ -535,7 +540,7 @@
             pltpu.VMEM((tiles, 2, slots * rows, TILE), bf16),
             pltpu.VMEM((tiles, 2, slots * rows, TILE), bf16),
             pltpu.VMEM((LINE * rows, hidden), bf16),
-            dma((2,)), dma, dma((4, slots, 2)), dma((slots, 2)),
+            dma, dma((DEPTH,)), dma, dma((4, slots, 2)), dma((slots, 2)),
             dma((slots, tiles)), dma((slots, tiles)),
             dma((2, 2, LINE - 1, PIECES)), dma((2, 2, LINE - 1, PIECES)),
             dma((LINE, PIECES)), dma((LINE, PIECES)),
@@ -544,7 +549,7 @@
         compiler_params=pltpu.CompilerParams(
             collective_id=0, has_side_effects=True, vmem_limit_bytes=67043328
         ),
-    )(ext, w_in, w_out)
+    )(tokens, routes.T, route_scores.T, placement, w_in, w_out)
 
 
 def on_device(tokens, routes, route_scores, placement, w_in, w_out):

time: 131 us -> 125 us (0.954)
  other arithmetic: 2.22 us -> 0 us
  local copies, waits for them, and re-layouts: 3.87 us -> 1.82 us
    concatenate x1 -> x0, local copies, waits for them, and re-layouts: 1.88 us -> none  [fused(): ext = jnp.concatenate([tokens, *thirds, filler], axis=1)]
    reduce_sum x3 -> x0, other arithmetic: 1.51 us -> none  [the longest x1 0.79 us: expert_weights(): jnp.sum(jnp.where(routes[:, :, None] == expert_ids, placement, 0), axis=-1)]
where the time goes in v4:
time: 125 us
  Pallas kernels  123 us (98%)
  local copies, waits for them, and re-layouts  1.82 us (1%)
    pallas_call x1, Pallas kernels, fused(): pl.pallas_call(layer_kernel, out_shape=jax.ShapeDtypeStruct((rows, cols),...  123 us

profile of v4, /device:TPU:8, one launch (start us, length us, event | category | flops | bytes accessed | tf_op | source)
XLA Modules:
  0.0 124.8 jit_solution(1244886534047304272)
XLA Ops:
  0.0 123.0 %shard_map.64 = bf16[64,3584]{1,0:T(8,128)(2,1)} custom-call(bf16[64,3584]{1,0:T(8,128)(2,1)} %tokens_ref.1, s32[8,64]{1,0:T(8,128)} %bitcast.2, f32[8,64]{1,0:T(8,128)} %bitcast.3, s32[16]{0:T(128)} %placement_ref.1, bf16[1,3584,2,1024]{3,2,1,0:T(2,128)(2,1)} %w_in_ref.1, bf16[1,1024,3584]{2,1,0:T(8,128)(2,1)} %w_out_ref.1), custom_call_target="tpu_custom_call" | custom-call | tf_op jit(solution)/shard_map/pallas_call | solution.py:516
  123.0 1.8 %copy.8 = bf16[64,3584]{1,0:T(8,128)(2,1)} copy(bf16[64,3584]{1,0:T(8,128)(2,1)} %shard_map.64) | data formatting | bytes 917504

commit v5 on v4

--- a/solution.py
+++ b/solution.py
@@ -224,9 +224,10 @@
             ship_along(plane, landed(slot_of(DIAGONAL, rank), h), DIAGONAL, rank, h)
         return act_on
 
-    def wait_for(line, rank):
-        for h in range(2):
+    def land(line, rank, h):
+        def act_on(plane):
             landed(slot_of(line, rank), h)
+        return act_on
 
     def sort_tile(ct):
         stage_copy(ct).wait()
@@ -316,12 +317,22 @@
             contrib.at[slot, :, cut(h)], target[0].at[target[1]].at[:, cut(h)],
             send.at[(*target[1], h)], recv.at[(*target[1], h)], chip))
 
+    def cross_on(rank, h):
+        def act_on(plane):
+            pass_sum(plane, h, slot_of(SIDE_B, rank), (a_in, (rank,)), a_send, a_recv, near_a)
+            pass_sum(plane, h, slot_of(SIDE_A, rank), (b_in, (rank,)), b_send, b_recv, near_b)
+        return act_on
+
+    def straight_on(h):
+        def act_on(plane):
+            pass_sum(plane, h, slot_of(SIDE_B, 0), (b_in, (0,)), b_send, b_recv, near_b)
+        return act_on
+
     def cross(rank, h):
-        pass_sum("all", h, slot_of(SIDE_B, rank), (a_in, (rank,)), a_send, a_recv, near_a)
-        pass_sum("all", h, slot_of(SIDE_A, rank), (b_in, (rank,)), b_send, b_recv, near_b)
+        cross_on(rank, h)("all")
 
     def straight(h):
-        pass_sum("all", h, slot_of(SIDE_B, 0), (b_in, (0,)), b_send, b_recv, near_b)
+        straight_on(h)("all")
 
     sends["all"] = []
 
@@ -362,10 +373,15 @@
             pass_sum(plane, h, slot, (b_in, (LINE,)), b_send, b_recv, near_b)
         return act_on
 
+    def turn_a_on(h):
+        def act_on(plane):
+            slot = slot_of(SIDE_A, 0)
+            add_up(h, contrib.at[slot], [contrib.at[slot], take(b_in, b_recv, (LINE,), h)])
+            pass_sum(plane, h, slot, (a_in, (0,)), a_send, a_recv, near_a)
+        return act_on
+
     def turn_a(h):
-        slot = slot_of(SIDE_A, 0)
-        add_up(h, contrib.at[slot], [contrib.at[slot], take(b_in, b_recv, (LINE,), h)])
-        pass_sum("all", h, slot, (a_in, (0,)), a_send, a_recv, near_a)
+        turn_a_on(h)("all")
 
     def finish(h):
         def act_on(plane):
@@ -394,102 +410,234 @@
     own_tokens.wait()
     on(EVERY, send_own)
     tiles_in = hidden // LANES
-    groups = ((0, 2), (2, 2), (4, 4), (8, 2), (10, 2), (12, 4))
-    for ct in range(tiles_in // 2):
-        sort_tile(ct)
-    on(EVERY, relay_side(0))
-    on(EVERY, pass_z(1, 0))
+    groups = ((0, 2), (2, 2), (4, 4), (8, 2), (10, 2), (12, 2), (14, 2))
+    sort_tile(0)
+    sort_tile(1)
+    sort_tile(2)
+    sort_tile(3)
+    on(INNER, pass_z(1, 0))
+    on(ENDS, pass_z(1, 0))
+    sort_tile(4)
+    sort_tile(5)
+    on(ENDS, land(SIDE_B, 0, 0))
+    on(INNER, relay_side(0))
     on(INNER, pass_z(2, 0))
-    for ct in range(tiles_in // 2, tiles_in):
-        sort_tile(ct)
-    on(EVERY, relay_side(1))
-    on(EVERY, pass_z(1, 1))
-    on(EVERY, pass_ab(1, 0))
-    on(EVERY, pass_ab(1, 1))
+    on(ENDS, pass_ab(1, 0))
+    on(INNER, pass_z(1, 1))
+    on(ENDS, relay_side(1))
+    on(INNER, pass_ab(1, 0))
+    on(ENDS, relay_side(0))
     on(INNER, pass_z(2, 1))
-    on(INNER, pass_ab(2, 0))
-    on(INNER, pass_ab(2, 1))
+    sort_tile(6)
+    on(ENDS, pass_z(1, 1))
+    on(INNER, relay_side(1))
+    on(ENDS, pass_ab(1, 1))
+    on(INNER, land(SIDE_B, 0, 0))
+    on(INNER, pass_z(3, 0))
+    sort_tile(7)
+    on(INNER, pass_ab(1, 1))
     feed(0)
-    on(INNER, pass_z(3, 0))
-    on(ENDS, relay_own(2, 0))
-    on(EVERY, relay_diagonal(0, 0))
     blend(0)
     out_weights.wait()
-    for h in every_piece:
-        close(0, h)
+    close(0, 2)
+    on(ENDS, land(SIDE_B, 0, 1))
+    on(INNER, pass_ab(2, 1))
+    on(ENDS, along(OWN, 1, 2))
+    close(0, 1)
+    on(ENDS, land(SIDE_B, 1, 0))
+    on(INNER, pass_ab(2, 0))
+    close(0, 0)
     on(INNER, pass_z(3, 1))
+    on(ENDS, relay_diagonal(0, 0))
+    on(ENDS, land(SIDE_A, 1, 1))
+    on(INNER, pass_ab(3, 1))
+    close(0, 3)
+    on(ENDS, pass_z(2, 0))
+    on(ENDS, land(SIDE_A, 1, 0))
+    on(INNER, land(SIDE_B, 0, 1))
+    on(ENDS, along(OWN, 1, 1))
     on(INNER, pass_ab(3, 0))
-    on(INNER, pass_ab(3, 1))
-    on(ENDS, relay_own(2, 1))
-    on(EVERY, relay_diagonal(0, 1))
-    for h in every_piece:
-        on(ENDS, along(OWN, 1, h))
-    wait_for(SIDE_B, 0)
+    on(ENDS, pass_ab(2, 0))
+    on(INNER, relay_diagonal(0, 0))
     feed(1)
+    on(ENDS, along(OWN, 1, 0))
+    on(ENDS, relay_diagonal(0, 1))
+    on(INNER, land(SIDE_B, 1, 0))
+    on(INNER, land(SIDE_B, 1, 1))
+    blend(1)
+    on(ENDS, land(SIDE_B, 1, 1))
+    close(1, 2)
+    on(ENDS, pass_z(2, 1))
+    on(ENDS, pass_ab(2, 1))
+    close(1, 3)
+    on(INNER, relay_diagonal(2, 0))
+    on(INNER, land(SIDE_A, 1, 1))
+    close(1, 0)
+    close(1, 1)
     on(INNER, relay_diagonal(1, 0))
-    on(ENDS, relay_own(3, 0))
-    blend(1)
-    for h in every_piece:
-        close(1, h)
-        straight(h)
-    on(ENDS, relay_own(3, 1))
+    on(INNER, relay_diagonal(0, 1))
+    on(ENDS, pass_z(3, 1))
+    on(ENDS, pass_ab(3, 1))
+    on(INNER, land(SIDE_A, 1, 0))
+    on(ENDS, pass_z(3, 0))
+    feed(2)
+    on(ENDS, pass_ab(3, 0))
+    blend(2)
+    on(INNER, straight_on(1))
+    close(2, 2)
+    on(ENDS, land(SIDE_A, 2, 0))
+    on(INNER, land(SIDE_A, 2, 1))
+    on(INNER, land(SIDE_B, 2, 0))
+    on(ENDS, land(SIDE_B, 2, 1))
+    on(INNER, land(SIDE_A, 3, 1))
+    close(2, 3)
+    on(ENDS, along(OWN, 2, 3))
+    close(2, 1)
+    on(ENDS, land(SIDE_B, 2, 0))
+    on(INNER, land(SIDE_B, 2, 1))
+    on(INNER, relay_diagonal(2, 1))
+    close(2, 0)
+    on(INNER, straight_on(2))
+    on(INNER, land(SIDE_A, 2, 0))
+    on(ENDS, land(SIDE_A, 2, 1))
+    on(ENDS, straight_on(1))
+    on(ENDS, along(OWN, 3, 1))
     on(INNER, relay_diagonal(1, 1))
-    on(INNER, relay_diagonal(2, 0))
-    wait_for(SIDE_A, 1)
-    wait_for(SIDE_B, 1)
-    feed(2)
-    on(INNER, relay_diagonal(2, 1))
+    on(ENDS, along(OWN, 1, 3))
+    feed(3)
+    on(ENDS, along(OWN, 2, 0))
+    on(INNER, straight_on(3))
+    on(ENDS, land(SIDE_A, 3, 1))
+    on(INNER, along(OWN, 2, 3))
+    blend(3)
+    on(ENDS, cross_on(1, 2))
+    on(ENDS, land(SIDE_A, 3, 0))
+    close(3, 1)
+    on(ENDS, land(DIAGONAL, 1, 1))
+    on(INNER, land(SIDE_B, 3, 1))
+    on(INNER, along(OWN, 3, 1))
+    close(3, 0)
+    on(ENDS, along(OWN, 3, 2))
+    on(INNER, cross_on(2, 1))
+    close(3, 2)
+    on(ENDS, land(DIAGONAL, 1, 0))
+    on(INNER, cross_on(1, 1))
+    on(ENDS, along(OWN, 2, 2))
+    on(INNER, land(SIDE_B, 3, 0))
+    on(INNER, relay_diagonal(3, 1))
+    on(INNER, land(SIDE_A, 3, 0))
+    on(ENDS, along(OWN, 3, 3))
+    on(ENDS, cross_on(2, 0))
+    on(ENDS, straight_on(2))
+    on(INNER, cross_on(1, 0))
+    on(ENDS, land(SIDE_B, 3, 0))
+    on(INNER, cross_on(2, 2))
+    on(ENDS, along(OWN, 2, 1))
+    on(ENDS, cross_on(1, 0))
+    on(ENDS, land(SIDE_B, 3, 1))
+    feed(4)
+    on(ENDS, land(DIAGONAL, 2, 0))
+    close(3, 3)
+    blend(4)
+    on(ENDS, along(OWN, 3, 0))
     on(INNER, relay_diagonal(3, 0))
-    blend(2)
-    for h in every_piece:
-        close(2, h)
-        cross(1, h)
-        on(ENDS, along(OWN, 3, h))
-        on(ENDS, along(OWN, 2, h))
-    on(INNER, relay_diagonal(3, 1))
-    wait_for(SIDE_A, 2)
-    wait_for(SIDE_B, 2)
-    feed(3)
-    blend(3)
-    for h in every_piece:
-        close(3, h)
-    wait_for(SIDE_A, 3)
-    wait_for(SIDE_B, 3)
-    feed(4)
-    for h in every_piece[:PIECES // 2]:
-        on(INNER, along(OWN, 3, h))
-    blend(4)
-    for h in every_piece[PIECES // 2:]:
-        on(INNER, along(OWN, 3, h))
-    for h in every_piece:
-        close(4, h)
-        cross(3, h)
-    for h in every_piece:
-        cross(2, h)
-    for rank in (1, 2, 3):
-        on(ENDS, lambda plane: wait_for(DIAGONAL, rank))
+    on(INNER, along(OWN, 2, 0))
+    close(4, 0)
+    on(INNER, cross_on(2, 0))
+    on(INNER, cross_on(3, 0))
+    on(INNER, along(OWN, 3, 2))
+    close(4, 1)
+    on(ENDS, cross_on(3, 0))
+    on(ENDS, cross_on(2, 1))
+    on(INNER, straight_on(0))
+    on(INNER, cross_on(3, 1))
     feed(5)
-    for h in every_piece:
-        on(INNER, along(OWN, 2, h))
-        on(INNER, along(OWN, 1, h))
+    on(ENDS, cross_on(3, 1))
+    close(4, 2)
+    close(4, 3)
+    on(INNER, along(OWN, 3, 3))
+    on(INNER, along(OWN, 1, 1))
     blend(5)
-    for h in every_piece:
-        close(5, h)
-        on(ENDS, along(DIAGONAL, 3, h))
-    for h in every_piece:
-        on(INNER, along(DIAGONAL, 3, h))
-    for h in every_piece:
-        on(ENDS, along(DIAGONAL, 2, h))
-        on(INNER, along(DIAGONAL, 1, h))
-    for h in every_piece:
-        on(ENDS, along(DIAGONAL, 1, h))
-        on(INNER, along(DIAGONAL, 2, h))
-    for h in every_piece:
-        on(EVERY, turn_b(h))
-    for h in every_piece:
-        turn_a(h)
-    for h in every_piece:
-        on(EVERY, finish(h))
+    on(ENDS, cross_on(3, 3))
+    close(5, 3)
+    close(5, 2)
+    close(5, 1)
+    on(INNER, along(OWN, 3, 0))
+    on(INNER, cross_on(3, 3))
+    on(ENDS, cross_on(1, 1))
+    on(INNER, along(OWN, 2, 2))
+    on(ENDS, along(DIAGONAL, 1, 2))
+    close(5, 0)
+    on(ENDS, cross_on(2, 2))
+    on(ENDS, cross_on(3, 2))
+    on(ENDS, land(DIAGONAL, 3, 1))
+    on(ENDS, along(DIAGONAL, 1, 0))
+    on(ENDS, land(DIAGONAL, 2, 1))
+    on(ENDS, land(DIAGONAL, 3, 0))
+    on(INNER, cross_on(2, 3))
+    feed(6)
+    on(ENDS, straight_on(0))
+    blend(6)
+    on(INNER, cross_on(3, 2))
+    close(6, 0)
+    on(ENDS, along(DIAGONAL, 3, 0))
+    on(INNER, along(DIAGONAL, 3, 0))
+    on(INNER, cross_on(1, 3))
+    on(INNER, along(OWN, 1, 0))
+    on(ENDS, along(DIAGONAL, 2, 0))
+    close(6, 3)
+    on(ENDS, along(DIAGONAL, 3, 3))
+    on(INNER, along(DIAGONAL, 2, 0))
+    on(INNER, along(DIAGONAL, 3, 3))
+    on(ENDS, straight_on(3))
+    on(INNER, along(DIAGONAL, 1, 0))
+    close(6, 1)
+    on(ENDS, along(DIAGONAL, 3, 1))
+    on(INNER, along(DIAGONAL, 3, 1))
+    on(INNER, along(DIAGONAL, 1, 3))
+    close(6, 2)
+    on(INNER, along(DIAGONAL, 3, 2))
+    on(ENDS, along(DIAGONAL, 3, 2))
+    on(INNER, cross_on(1, 2))
+    on(INNER, along(DIAGONAL, 1, 1))
+    on(INNER, turn_b(0))
+    on(INNER, along(DIAGONAL, 2, 2))
+    on(ENDS, along(DIAGONAL, 2, 2))
+    on(INNER, along(DIAGONAL, 1, 2))
+    on(ENDS, turn_b(0))
+    on(INNER, along(DIAGONAL, 2, 1))
+    on(INNER, along(DIAGONAL, 2, 3))
+    on(INNER, turn_a_on(0))
+    on(INNER, along(OWN, 2, 1))
+    on(ENDS, along(DIAGONAL, 2, 1))
+    on(ENDS, cross_on(2, 3))
+    on(ENDS, along(DIAGONAL, 2, 3))
+    on(INNER, turn_b(2))
+    on(INNER, along(OWN, 1, 2))
+    on(ENDS, along(DIAGONAL, 1, 1))
+    on(INNER, along(OWN, 1, 3))
+    on(ENDS, cross_on(1, 3))
+    on(INNER, turn_b(1))
+    on(ENDS, turn_a_on(0))
+    on(INNER, turn_a_on(2))
+    on(INNER, finish(0))
+    on(ENDS, turn_b(3))
+    on(INNER, turn_b(3))
+    on(ENDS, along(DIAGONAL, 1, 3))
+    on(ENDS, turn_b(1))
+    on(INNER, turn_a_on(1))
+    on(ENDS, turn_a_on(3))
+    on(INNER, turn_a_on(3))
+    on(ENDS, turn_b(2))
+    on(ENDS, turn_a_on(1))
+    on(ENDS, turn_a_on(2))
+    on(ENDS, finish(0))
+    on(INNER, finish(1))
+    on(INNER, finish(2))
+    on(ENDS, finish(1))
+    on(INNER, finish(3))
+    on(ENDS, finish(3))
+    on(ENDS, finish(2))
     for copy in sends["all"]:
         copy().wait_send()
 

time: 125 us -> 117 us (0.936)
  Pallas kernels: 123 us -> 115 us
    pallas_call x1, Pallas kernels: 123 us -> 115 us  [fused(): pl.pallas_call(layer_kernel, out_shape=jax.ShapeDtypeStruct((rows, cols),...]
where the time goes in v5:
time: 117 us
  Pallas kernels  115 us (98%)
  local copies, waits for them, and re-layouts  1.82 us (2%)
    pallas_call x1, Pallas kernels, fused(): pl.pallas_call(layer_kernel, out_shape=jax.ShapeDtypeStruct((rows, cols),...  115 us

profile of v5, /device:TPU:8, one launch (start us, length us, event | category | flops | bytes accessed | tf_op | source)
XLA Modules:
  0.0 117.0 jit_solution(9429926960287179279)
XLA Ops:
  0.0 115.2 %shard_map.64 = bf16[64,3584]{1,0:T(8,128)(2,1)} custom-call(bf16[64,3584]{1,0:T(8,128)(2,1)} %tokens_ref.1, s32[8,64]{1,0:T(8,128)} %bitcast.2, f32[8,64]{1,0:T(8,128)} %bitcast.3, s32[16]{0:T(128)} %placement_ref.1, bf16[1,3584,2,1024]{3,2,1,0:T(2,128)(2,1)} %w_in_ref.1, bf16[1,1024,3584]{2,1,0:T(8,128)(2,1)} %w_out_ref.1), custom_call_target="tpu_custom_call" | custom-call | tf_op jit(solution)/shard_map/pallas_call | solution.py:664
  115.2 1.8 %copy.8 = bf16[64,3584]{1,0:T(8,128)(2,1)} copy(bf16[64,3584]{1,0:T(8,128)(2,1)} %shard_map.64) | data formatting | bytes 917504

commit v6 on v5

--- a/solution.py
+++ b/solution.py
@@ -419,29 +419,29 @@
     on(ENDS, pass_z(1, 0))
     sort_tile(4)
     sort_tile(5)
+    on(INNER, pass_z(2, 0))
     on(ENDS, land(SIDE_B, 0, 0))
     on(INNER, relay_side(0))
-    on(INNER, pass_z(2, 0))
     on(ENDS, pass_ab(1, 0))
     on(INNER, pass_z(1, 1))
     on(ENDS, relay_side(1))
     on(INNER, pass_ab(1, 0))
     on(ENDS, relay_side(0))
+    on(INNER, relay_side(1))
     on(INNER, pass_z(2, 1))
     sort_tile(6)
     on(ENDS, pass_z(1, 1))
-    on(INNER, relay_side(1))
     on(ENDS, pass_ab(1, 1))
     on(INNER, land(SIDE_B, 0, 0))
     on(INNER, pass_z(3, 0))
     sort_tile(7)
     on(INNER, pass_ab(1, 1))
+    on(INNER, pass_ab(2, 1))
     feed(0)
     blend(0)
     out_weights.wait()
     close(0, 2)
     on(ENDS, land(SIDE_B, 0, 1))
-    on(INNER, pass_ab(2, 1))
     on(ENDS, along(OWN, 1, 2))
     close(0, 1)
     on(ENDS, land(SIDE_B, 1, 0))
@@ -462,6 +462,7 @@
     feed(1)
     on(ENDS, along(OWN, 1, 0))
     on(ENDS, relay_diagonal(0, 1))
+    on(INNER, relay_diagonal(0, 1))
     on(INNER, land(SIDE_B, 1, 0))
     on(INNER, land(SIDE_B, 1, 1))
     blend(1)
@@ -475,7 +476,6 @@
     close(1, 0)
     close(1, 1)
     on(INNER, relay_diagonal(1, 0))
-    on(INNER, relay_diagonal(0, 1))
     on(ENDS, pass_z(3, 1))
     on(ENDS, pass_ab(3, 1))
     on(INNER, land(SIDE_A, 1, 0))
@@ -487,25 +487,25 @@
     close(2, 2)
     on(ENDS, land(SIDE_A, 2, 0))
     on(INNER, land(SIDE_A, 2, 1))
+    on(ENDS, land(SIDE_B, 2, 1))
+    close(2, 3)
     on(INNER, land(SIDE_B, 2, 0))
-    on(ENDS, land(SIDE_B, 2, 1))
     on(INNER, land(SIDE_A, 3, 1))
-    close(2, 3)
     on(ENDS, along(OWN, 2, 3))
     close(2, 1)
+    on(INNER, straight_on(2))
     on(ENDS, land(SIDE_B, 2, 0))
+    on(INNER, relay_diagonal(2, 1))
     on(INNER, land(SIDE_B, 2, 1))
-    on(INNER, relay_diagonal(2, 1))
     close(2, 0)
-    on(INNER, straight_on(2))
-    on(INNER, land(SIDE_A, 2, 0))
     on(ENDS, land(SIDE_A, 2, 1))
-    on(ENDS, straight_on(1))
     on(ENDS, along(OWN, 3, 1))
     on(INNER, relay_diagonal(1, 1))
+    on(INNER, land(SIDE_A, 2, 0))
     on(ENDS, along(OWN, 1, 3))
     feed(3)
     on(ENDS, along(OWN, 2, 0))
+    on(ENDS, straight_on(1))
     on(INNER, straight_on(3))
     on(ENDS, land(SIDE_A, 3, 1))
     on(INNER, along(OWN, 2, 3))
@@ -514,28 +514,28 @@
     on(ENDS, land(SIDE_A, 3, 0))
     close(3, 1)
     on(ENDS, land(DIAGONAL, 1, 1))
-    on(INNER, land(SIDE_B, 3, 1))
     on(INNER, along(OWN, 3, 1))
-    close(3, 0)
-    on(ENDS, along(OWN, 3, 2))
     on(INNER, cross_on(2, 1))
     close(3, 2)
     on(ENDS, land(DIAGONAL, 1, 0))
     on(INNER, cross_on(1, 1))
+    close(3, 0)
+    on(ENDS, along(OWN, 3, 2))
     on(ENDS, along(OWN, 2, 2))
-    on(INNER, land(SIDE_B, 3, 0))
-    on(INNER, relay_diagonal(3, 1))
+    on(INNER, land(SIDE_B, 3, 1))
     on(INNER, land(SIDE_A, 3, 0))
     on(ENDS, along(OWN, 3, 3))
     on(ENDS, cross_on(2, 0))
+    on(ENDS, land(SIDE_B, 3, 0))
+    on(ENDS, along(OWN, 2, 1))
+    on(ENDS, cross_on(1, 0))
+    on(INNER, land(SIDE_B, 3, 0))
+    on(INNER, relay_diagonal(3, 1))
+    on(INNER, cross_on(2, 2))
+    on(ENDS, land(SIDE_B, 3, 1))
+    feed(4)
     on(ENDS, straight_on(2))
     on(INNER, cross_on(1, 0))
-    on(ENDS, land(SIDE_B, 3, 0))
-    on(INNER, cross_on(2, 2))
-    on(ENDS, along(OWN, 2, 1))
-    on(ENDS, cross_on(1, 0))
-    on(ENDS, land(SIDE_B, 3, 1))
-    feed(4)
     on(ENDS, land(DIAGONAL, 2, 0))
     close(3, 3)
     blend(4)
@@ -549,22 +549,23 @@
     close(4, 1)
     on(ENDS, cross_on(3, 0))
     on(ENDS, cross_on(2, 1))
+    feed(5)
+    on(ENDS, cross_on(3, 1))
+    on(INNER, cross_on(2, 3))
+    close(4, 2)
     on(INNER, straight_on(0))
     on(INNER, cross_on(3, 1))
-    feed(5)
-    on(ENDS, cross_on(3, 1))
-    close(4, 2)
     close(4, 3)
     on(INNER, along(OWN, 3, 3))
     on(INNER, along(OWN, 1, 1))
+    on(ENDS, cross_on(3, 3))
     blend(5)
-    on(ENDS, cross_on(3, 3))
     close(5, 3)
     close(5, 2)
     close(5, 1)
     on(INNER, along(OWN, 3, 0))
+    on(ENDS, cross_on(1, 1))
     on(INNER, cross_on(3, 3))
-    on(ENDS, cross_on(1, 1))
     on(INNER, along(OWN, 2, 2))
     on(ENDS, along(DIAGONAL, 1, 2))
     close(5, 0)
@@ -574,7 +575,6 @@
     on(ENDS, along(DIAGONAL, 1, 0))
     on(ENDS, land(DIAGONAL, 2, 1))
     on(ENDS, land(DIAGONAL, 3, 0))
-    on(INNER, cross_on(2, 3))
     feed(6)
     on(ENDS, straight_on(0))
     blend(6)
@@ -589,6 +589,7 @@
     on(ENDS, along(DIAGONAL, 3, 3))
     on(INNER, along(DIAGONAL, 2, 0))
     on(INNER, along(DIAGONAL, 3, 3))
+    on(ENDS, cross_on(2, 3))
     on(ENDS, straight_on(3))
     on(INNER, along(DIAGONAL, 1, 0))
     close(6, 1)
@@ -604,13 +605,12 @@
     on(INNER, along(DIAGONAL, 2, 2))
     on(ENDS, along(DIAGONAL, 2, 2))
     on(INNER, along(DIAGONAL, 1, 2))
-    on(ENDS, turn_b(0))
     on(INNER, along(DIAGONAL, 2, 1))
     on(INNER, along(DIAGONAL, 2, 3))
     on(INNER, turn_a_on(0))
     on(INNER, along(OWN, 2, 1))
     on(ENDS, along(DIAGONAL, 2, 1))
-    on(ENDS, cross_on(2, 3))
+    on(ENDS, turn_b(0))
     on(ENDS, along(DIAGONAL, 2, 3))
     on(INNER, turn_b(2))
     on(INNER, along(OWN, 1, 2))
@@ -621,11 +621,11 @@
     on(ENDS, turn_a_on(0))
     on(INNER, turn_a_on(2))
     on(INNER, finish(0))
+    on(ENDS, along(DIAGONAL, 1, 3))
     on(ENDS, turn_b(3))
     on(INNER, turn_b(3))
-    on(ENDS, along(DIAGONAL, 1, 3))
+    on(INNER, turn_a_on(1))
     on(ENDS, turn_b(1))
-    on(INNER, turn_a_on(1))
     on(ENDS, turn_a_on(3))
     on(INNER, turn_a_on(3))
     on(ENDS, turn_b(2))

time: 117 us -> 116 us (level); the launches traced: 117 us -> 115 us
  Pallas kernels: 115 us -> 113 us
    pallas_call x1, Pallas kernels: 115 us -> 113 us  [fused(): pl.pallas_call(layer_kernel, out_shape=jax.ShapeDtypeStruct((rows, cols),...]
where the time goes in v6:
time: 116 us; the launch traced here: 115 us
  Pallas kernels  113 us (97%)
  local copies, waits for them, and re-layouts  1.82 us (2%)
    pallas_call x1, Pallas kernels, fused(): pl.pallas_call(layer_kernel, out_shape=jax.ShapeDtypeStruct((rows, cols),...  113 us

profile of v6, /device:TPU:8, one launch (start us, length us, event | category | flops | bytes accessed | tf_op | source)
XLA Modules:
  0.0 114.8 jit_solution(514163508595795205)
XLA Ops:
  0.0 112.9 %shard_map.64 = bf16[64,3584]{1,0:T(8,128)(2,1)} custom-call(bf16[64,3584]{1,0:T(8,128)(2,1)} %tokens_ref.1, s32[8,64]{1,0:T(8,128)} %bitcast.2, f32[8,64]{1,0:T(8,128)} %bitcast.3, s32[16]{0:T(128)} %placement_ref.1, bf16[1,3584,2,1024]{3,2,1,0:T(2,128)(2,1)} %w_in_ref.1, bf16[1,1024,3584]{2,1,0:T(8,128)(2,1)} %w_out_ref.1), custom_call_target="tpu_custom_call" | custom-call | tf_op jit(solution)/shard_map/pallas_call | solution.py:664
  112.9 1.8 %copy.8 = bf16[64,3584]{1,0:T(8,128)(2,1)} copy(bf16[64,3584]{1,0:T(8,128)(2,1)} %shard_map.64) | data formatting | bytes 917504
